TPU v7x, 32 devices: a whole 2x2x4 slice. The times are simulated.
32 devices in a mesh: gx: 8 (over z, core), gy: 4 (over y, x).
Axes of the slice: x: 2, y: 2, z: 4, core: 2. Of those that a mesh axis runs over, the one named last changes fastest.
Arguments:
- features: bfloat16 [32, 64, 32, 128], P(None, 'gx', 'gy'), may hold values from -6 to 6
- occupancy: int32 [8, 4, 16], replicated, may hold values 0 or 1
- weight_one: bfloat16 [32, 3, 3, 3, 32], replicated, may hold values from -0.21875 to 0.21875
- bias_one: float32 [32], replicated, may hold values from -3 to 3
- weight_two: bfloat16 [32, 3, 3, 3, 32], replicated, may hold values from -0.21875 to 0.21875
- bias_two: float32 [32], replicated, may hold values from -3 to 3
- grad_pooled: bfloat16 [32, 32, 16, 64], P(None, 'gx', 'gy'), may hold values from -24 to 24
- pool_choice: int32 [32, 32, 16, 64], P(None, 'gx', 'gy'), may hold values from 0 to 7
Outputs:
- grad_input: bfloat16 [32, 64, 32, 128], P(None, 'gx', 'gy')
- grad_weight_one: float32 [32, 3, 3, 3, 32], replicated
- grad_bias_one: float32 [32], replicated
- grad_weight_two: float32 [32, 3, 3, 3, 32], replicated
- grad_bias_two: float32 [32], replicated
All inputs are finite; a program needn't handle non-finite values.
Results may differ from a plain program's by a relative error of at most 0.035.
The roundings to bfloat16 on the way count: a program that leaves them out, or rounds other values in their place, can miss the bound.
Values may be sent and summed in bfloat16 or wider, within the bound.
A program may use at most 64 MiB of HBM per device.

v0:
```python
import math

import jax
import jax.numpy as jnp
from jax import lax
from jax.sharding import PartitionSpec as P


def padded_2(x, sides, width):
    for axis, dim in sides:
        devices, length = (lax.axis_size(axis), x.shape[dim])
        up = [(i, (i + 1) % devices) for i in range(devices - 1)]
        down = [(j, i) for i, j in up]
        last = lax.slice_in_dim(x, length - width, length, axis=dim)
        first = lax.slice_in_dim(x, 0, width, axis=dim)
        before = lax.ppermute(last, axis, up)
        after = lax.ppermute(first, axis, down)
        x = jnp.concatenate([before, x, after], axis=dim)
    return x


def depth_stack(padded):
    depth = padded.shape[3]
    framed = jnp.pad(padded, ((0, 0), (0, 0), (0, 0), (1, 1)))
    return jnp.concatenate(
        [framed[..., 0:depth], framed[..., 1 : depth + 1], framed[..., 2 : depth + 2]], axis=0
    )


def convolve(stacked, weight):
    width_x = stacked.shape[1] - 2
    width_y = stacked.shape[2] - 2
    channels = weight.shape[0]
    total = None
    for row_off in range(3):
        for col_off in range(3):
            kernel = weight[:, row_off, col_off].reshape(channels, -1)
            window = stacked[:, row_off : row_off + width_x, col_off : col_off + width_y, :]
            term = jnp.einsum("ok,kxyz->oxyz", kernel, window, preferred_element_type=jnp.float32)
            total = term if total is None else total + term
    return total


def weight_grad(upstream, stacked):
    width_x = upstream.shape[1]
    width_y = upstream.shape[2]
    channels = upstream.shape[0]
    blocks = []
    for row_off in range(3):
        column_parts = []
        for col_off in range(3):
            window = stacked[:, row_off : row_off + width_x, col_off : col_off + width_y, :]
            part = jnp.einsum("oxyz,kxyz->ok", upstream, window, preferred_element_type=jnp.float32)
            column_parts.append(part.reshape(channels, 3, -1))
        blocks.append(jnp.stack(column_parts, axis=1))
    return jnp.stack(blocks, axis=1)


def flipped(weight):
    return jnp.flip(weight, (1, 2, 3)).transpose(4, 1, 2, 3, 0)


def expand(field, factor):
    return jnp.repeat(
        jnp.repeat(jnp.repeat(field, factor, axis=-3), factor, axis=-2), factor, axis=-1
    )


def body(features, occupancy, weight_one, bias_one, weight_two, bias_two, grad_pooled, pool_choice):
    cells_x = features.shape[1]
    cells_y = features.shape[2]
    cells_z = features.shape[3]
    brick_x = cells_x // 8
    brick_y = cells_y // 8
    padded_flags = jnp.pad(occupancy, ((1, 1), (1, 1), (0, 0)))
    corner_x = lax.axis_index("gx") * brick_x
    corner_y = lax.axis_index("gy") * brick_y
    flag_window = lax.dynamic_slice(
        padded_flags,
        (corner_x, corner_y, jnp.int32(0)),
        (brick_x + 2, brick_y + 2, occupancy.shape[2]),
    )
    cell_flags = expand(flag_window, 8).astype(jnp.float32)
    mask_inner = cell_flags[8 : 8 + cells_x, 8 : 8 + cells_y]
    masked = (features.astype(jnp.float32) * mask_inner).astype(jnp.bfloat16)
    input_padded = padded_2(masked, (("gx", 1), ("gy", 2)), 1)
    input_stack = depth_stack(input_padded)
    pre_one = convolve(input_stack, weight_one) + bias_one[:, None, None, None]
    hidden = (jnp.maximum(pre_one, 0.0) * mask_inner).astype(jnp.bfloat16)
    hidden_padded = padded_2(hidden, (("gx", 1), ("gy", 2)), 1)
    hidden_stack = depth_stack(hidden_padded)
    pre_two = convolve(hidden_stack, weight_two) + bias_two[:, None, None, None]
    spread = expand(grad_pooled.astype(jnp.float32), 2)
    chosen = expand(pool_choice, 2)
    shape_cells = (cells_x, cells_y, cells_z)
    parity = (
        4 * (lax.broadcasted_iota(jnp.int32, shape_cells, 0) % 2)
        + 2 * (lax.broadcasted_iota(jnp.int32, shape_cells, 1) % 2)
        + lax.broadcasted_iota(jnp.int32, shape_cells, 2) % 2
    )
    upstream = jnp.where(chosen == parity[None], spread, 0.0)
    delta_two = (upstream * (pre_two > 0).astype(jnp.float32) * mask_inner).astype(jnp.bfloat16)
    local_w_two = weight_grad(delta_two, hidden_stack)
    local_b_two = jnp.sum(delta_two.astype(jnp.float32), axis=(1, 2, 3))
    delta_two_padded = padded_2(delta_two, (("gx", 1), ("gy", 2)), 1)
    back_one = convolve(depth_stack(delta_two_padded), flipped(weight_two))
    delta_one = (back_one * (pre_one > 0).astype(jnp.float32) * mask_inner).astype(jnp.bfloat16)
    local_w_one = weight_grad(delta_one, input_stack)
    local_b_one = jnp.sum(delta_one.astype(jnp.float32), axis=(1, 2, 3))
    summed_w_one, summed_b_one, summed_w_two, summed_b_two = lax.psum(
        (local_w_one, local_b_one, local_w_two, local_b_two), ("gx", "gy")
    )
    delta_one_padded = padded_2(delta_one, (("gx", 1), ("gy", 2)), 1)
    back_input = convolve(depth_stack(delta_one_padded), flipped(weight_one))
    grad_input = (back_input * mask_inner).astype(jnp.bfloat16)
    total_cells = cells_x * lax.axis_size("gx") * cells_y * lax.axis_size("gy") * cells_z
    scale = 1.0 / math.sqrt(total_cells)
    return (
        grad_input,
        summed_w_one * scale,
        summed_b_one * scale,
        summed_w_two * scale,
        summed_b_two * scale,
    )


def solution(mesh):
    placed = (
        P(None, "gx", "gy", None),
        P(),
        P(),
        P(),
        P(),
        P(),
        P(None, "gx", "gy", None),
        P(None, "gx", "gy", None),
    )
    return jax.shard_map(
        body,
        mesh=mesh,
        in_specs=placed,
        out_specs=(P(None, "gx", "gy", None), P(), P(), P(), P()),
        check_vma=False,
    )
```

profile of v0, /device:TPU:0, one launch (start us, length us, event | category | flops | bytes accessed | tf_op | source)
XLA Modules:
  0.0 320.6 jit_solution(16810136861805906522)
XLA Ops:
  9.3 1.3 collective-permute-start.1
  10.6 3.0 collective-permute-start
  16.9 1.3 collective-permute-start.3
  18.2 5.5 %collective-permute-start.2 = (bf16[32,10,1,128]{3,0,2,1:T(8,128)(2,1)S(1)}, bf16[32,10,1,128]{3,0,2,1:T(8,128)(2,1)S(1)}, u32[]{:S(2)}, u32[]{:S(2)}) collective-permute-start(bf16[32,10,1,128]{3,0,2,1:T(8,128)(2,1)S(1)} %get-tuple-element.45), channel_id=1, source_target_pairs={{0,1},{1,2},{2,3},{4,5},{5,6},{6,7},{8,9},{9,10},{10,11},{12,13},{... | collective-permute-start | bytes 245768 | tf_op jit(solution)/shard_map/ppermute | solution.py:16
  24.3 1.7 collective-permute-done.2
  26.1 1.5 fusion.20
  33.6 1.3 collective-permute-start.5
  34.9 3.1 collective-permute-start.4
  39.6 1.3 collective-permute-start.7
  40.9 6.4 %collective-permute-start.6 = (bf16[32,10,1,128]{3,0,2,1:T(8,128)(2,1)}, bf16[32,10,1,128]{3,0,2,1:T(8,128)(2,1)}, u32[]{:S(2)}, u32[]{:S(2)}) collective-permute-start(bf16[32,10,1,128]{3,0,2,1:T(8,128)(2,1)} %get-tuple-element.43), channel_id=1, source_target_pairs={{0,1},{1,2},{2,3},{4,5},{5,6},{6,7},{8,9},{9,10},{10,11},{12,13},{... | collective-permute-start | bytes 245768 | tf_op jit(solution)/shard_map/ppermute | solution.py:16
  50.1 2.3 broadcast_in_dim.48
  52.4 3.6 %copy.193 = f32[32,8,8,128]{3,0,2,1:T(8,128)} copy(f32[32,8,8,128]{0,2,3,1:T(8,128)} %bitcast.296) | data formatting | bytes 2097152 | tf_op jit(solution)/shard_map/reshape | solution.py:64
  58.0 2.3 broadcast_in_dim.45
  60.4 3.8 %copy.191 = s32[32,8,8,128]{3,0,2,1:T(8,128)} copy(s32[32,8,8,128]{0,2,3,1:T(8,128)} %bitcast.297) | data formatting | bytes 2097152 | tf_op jit(solution)/shard_map/reshape | solution.py:64
  65.2 2.4 fusion.26
  68.1 1.5 pad_maximum_fusion.1
  73.2 1.5 convert_reduce_fusion
  78.6 1.3 fusion.303
  83.0 1.3 collective-permute-start.9
  84.3 3.9 %collective-permute-start.8 = (bf16[32,1,8,128]{3,0,2,1:T(8,128)(2,1)}, bf16[32,1,8,128]{3,0,2,1:T(8,128)(2,1)S(1)}, u32[]{:S(2)}, u32[]{:S(2)}) collective-permute-start(bf16[32,1,8,128]{3,0,2,1:T(8,128)(2,1)} %get-tuple-element.49), channel_id=1, source_target_pairs={{0,4},{4,8},{8,12},{12,16},{16,20},{20,24},{24,28},{1,5},{5,9},{9,... | collective-permute-start | bytes 196616 | tf_op jit(solution)/shard_map/ppermute | solution.py:16
  89.5 1.4 stack_reshape.65
  91.0 1.4 stack_reshape.64
  94.2 1.5 collective-permute-start.11
  95.8 5.5 %collective-permute-start.10 = (bf16[32,10,1,128]{3,0,2,1:T(8,128)(2,1)S(1)}, bf16[32,10,1,128]{3,0,2,1:T(8,128)(2,1)S(1)}, u32[]{:S(2)}, u32[]{:S(2)}) collective-permute-start(bf16[32,10,1,128]{3,0,2,1:T(8,128)(2,1)S(1)} %get-tuple-element.41), channel_id=1, source_target_pairs={{0,1},{1,2},{2,3},{4,5},{5,6},{6,7},{8,9},{9,10},{10,11},{12,13},{... | collective-permute-start | bytes 245768 | tf_op jit(solution)/shard_map/ppermute | solution.py:16
  103.3 1.5 fusion.24
  116.8 1.3 collective-permute-start.13
  118.1 4.3 %collective-permute-start.12 = (bf16[32,1,8,128]{3,0,2,1:T(8,128)(2,1)S(1)}, bf16[32,1,8,128]{3,0,2,1:T(8,128)(2,1)S(1)}, u32[]{:S(2)}, u32[]{:S(2)}) collective-permute-start(bf16[32,1,8,128]{3,0,2,1:T(8,128)(2,1)S(1)} %get-tuple-element.47), channel_id=1, source_target_pairs={{0,4},{4,8},{8,12},{12,16},{16,20},{20,24},{24,28},{1,5},{5,9},{9,... | collective-permute-start | bytes 196616 | tf_op jit(solution)/shard_map/ppermute | solution.py:16
  123.3 44.2 %all-reduce.5 = (f32[32]{0:T(128)S(1)}, f32[32]{0:T(128)S(1)}) all-reduce(f32[32]{0:T(128)S(1)} %get-tuple-element.29, f32[32]{0:T(128)S(1)} %copy-done.41), channel_id=1, replica_groups=mesh['gx'=8,'gy'=4] {'gx','gy'}, use_global_device_ids=true, to_apply=%region_2.3 | all-reduce | flops 64 | bytes 512 | tf_op jit(solution)/shard_map/psum | solution.py:110
  169.7 1.3 collective-permute-start.15
  171.0 5.1 %collective-permute-start.14 = (bf16[32,10,1,128]{3,0,2,1:T(8,128)(2,1)S(1)}, bf16[32,10,1,128]{3,0,2,1:T(8,128)(2,1)S(1)}, u32[]{:S(2)}, u32[]{:S(2)}) collective-permute-start(bf16[32,10,1,128]{3,0,2,1:T(8,128)(2,1)S(1)} %get-tuple-element.39), channel_id=1, source_target_pairs={{0,1},{1,2},{2,3},{4,5},{5,6},{6,7},{8,9},{9,10},{10,11},{12,13},{... | collective-permute-start | bytes 245768 | tf_op jit(solution)/shard_map/ppermute | solution.py:16
  176.1 125.6 %all-reduce.9.cloned.1.call-done = (f32[32,3,3,3,32]{4,3,0,2,1:T(4,128)}, f32[32,3,3,3,32]{4,3,0,2,1:T(4,128)}) async-done(((f32[32,3,3,3,32]{4,3,0,2,1:T(4,128)}, f32[32,3,3,3,32]{4,3,0,2,1:T(4,128)}), (f32[32,3,3,3,32]{4,3,0,2,1:T(4,128)}, f32[32,3,3,3,32]{4,3,0,2,1:T(4,128)})) %all-reduce.9.cloned.1.call-update) | async-done | bytes 221200 | tf_op jit(solution)/shard_map/psum | solution.py:110
  305.8 1.5 select_maximum_fusion
  (263 shorter events, 60.4 us)
Async XLA Ops:
  7.2 294.5 %all-reduce.9.cloned.1.call-start = ((), (), s32[]{:S(2)}) async-start(), calls=%async_computation | async-start | bytes 2359296 | tf_op jit(solution)/shard_map/psum | solution.py:110
  8.3 5.3 %copy-start.4 = (bf16[32,3,3,3,32]{4,0,3,2,1:T(8,128)(2,1)S(1)}, bf16[32,3,3,3,32]{4,0,3,2,1:T(8,128)(2,1)}, u32[]{:S(2)}) copy-start(bf16[32,3,3,3,32]{4,0,3,2,1:T(8,128)(2,1)} %param.10) | copy-start | bytes 165892
  8.3 5.4 %copy-start.5 = (bf16[32,3,3,3,32]{4,0,3,2,1:T(8,128)(2,1)S(1)}, bf16[32,3,3,3,32]{4,0,3,2,1:T(8,128)(2,1)}, u32[]{:S(2)}) copy-start(bf16[32,3,3,3,32]{4,0,3,2,1:T(8,128)(2,1)} %param.12) | copy-start | bytes 165892
  9.3 7.6 %collective-permute-start.1 = (bf16[32,1,8,128]{3,0,2,1:T(8,128)(2,1)S(1)}, bf16[32,1,8,128]{3,0,2,1:T(8,128)(2,1)S(1)}, u32[]{:S(2)}, u32[]{:S(2)}) collective-permute-start(bf16[32,1,8,128]{3,0,2,1:T(8,128)(2,1)S(1)} %get-tuple-element.54), channel_id=1, source_target_pairs={{4,0},{8,4},{12,8},{16,12},{20,16},{24,20},{28,24},{5,1},{9,5},{13... | collective-permute-start | bytes 196616 | tf_op jit(solution)/shard_map/ppermute | solution.py:17
  10.6 6.3 %collective-permute-start = (bf16[32,1,8,128]{3,0,2,1:T(8,128)(2,1)S(1)}, bf16[32,1,8,128]{3,0,2,1:T(8,128)(2,1)S(1)}, u32[]{:S(2)}, u32[]{:S(2)}) collective-permute-start(bf16[32,1,8,128]{3,0,2,1:T(8,128)(2,1)S(1)} %get-tuple-element.53), channel_id=1, source_target_pairs={{0,4},{4,8},{8,12},{12,16},{16,20},{20,24},{24,28},{1,5},{5,9},{9,... | collective-permute-start | bytes 196616 | tf_op jit(solution)/shard_map/ppermute | solution.py:16
  16.9 7.4 %collective-permute-start.3 = (bf16[32,10,1,128]{3,0,2,1:T(8,128)(2,1)S(1)}, bf16[32,10,1,128]{3,0,2,1:T(8,128)(2,1)S(1)}, u32[]{:S(2)}, u32[]{:S(2)}) collective-permute-start(bf16[32,10,1,128]{3,0,2,1:T(8,128)(2,1)S(1)} %get-tuple-element.46), channel_id=1, source_target_pairs={{1,0},{2,1},{3,2},{5,4},{6,5},{7,6},{9,8},{10,9},{11,10},{13,12},{... | collective-permute-start | bytes 245768 | tf_op jit(solution)/shard_map/ppermute | solution.py:17
  18.2 7.8 %collective-permute-start.2 = (bf16[32,10,1,128]{3,0,2,1:T(8,128)(2,1)S(1)}, bf16[32,10,1,128]{3,0,2,1:T(8,128)(2,1)S(1)}, u32[]{:S(2)}, u32[]{:S(2)}) collective-permute-start(bf16[32,10,1,128]{3,0,2,1:T(8,128)(2,1)S(1)} %get-tuple-element.45), channel_id=1, source_target_pairs={{0,1},{1,2},{2,3},{4,5},{5,6},{6,7},{8,9},{9,10},{10,11},{12,13},{... | collective-permute-start | bytes 245768 | tf_op jit(solution)/shard_map/ppermute | solution.py:16
  33.6 4.4 %collective-permute-start.5 = (bf16[32,1,8,128]{3,0,2,1:T(8,128)(2,1)S(1)}, bf16[32,1,8,128]{3,0,2,1:T(8,128)(2,1)S(1)}, u32[]{:S(2)}, u32[]{:S(2)}) collective-permute-start(bf16[32,1,8,128]{3,0,2,1:T(8,128)(2,1)S(1)} %get-tuple-element.52), channel_id=1, source_target_pairs={{4,0},{8,4},{12,8},{16,12},{20,16},{24,20},{28,24},{5,1},{9,5},{13... | collective-permute-start | bytes 196616 | tf_op jit(solution)/shard_map/ppermute | solution.py:17
  34.9 4.0 %collective-permute-start.4 = (bf16[32,1,8,128]{3,0,2,1:T(8,128)(2,1)S(1)}, bf16[32,1,8,128]{3,0,2,1:T(8,128)(2,1)S(1)}, u32[]{:S(2)}, u32[]{:S(2)}) collective-permute-start(bf16[32,1,8,128]{3,0,2,1:T(8,128)(2,1)S(1)} %get-tuple-element.51), channel_id=1, source_target_pairs={{0,4},{4,8},{8,12},{12,16},{16,20},{20,24},{24,28},{1,5},{5,9},{9,... | collective-permute-start | bytes 196616 | tf_op jit(solution)/shard_map/ppermute | solution.py:16
  38.0 9.3 %copy-start.6 = (bf16[32,1,8,128]{3,0,2,1:T(8,128)(2,1)}, bf16[32,1,8,128]{3,0,2,1:T(8,128)(2,1)S(1)}, u32[]{:S(2)}) copy-start(bf16[32,1,8,128]{3,0,2,1:T(8,128)(2,1)S(1)} %collective-permute-done.5) | copy-start | bytes 196612
  38.9 8.4 %copy-start.8 = (bf16[32,1,8,128]{3,0,2,1:T(8,128)(2,1)}, bf16[32,1,8,128]{3,0,2,1:T(8,128)(2,1)S(1)}, u32[]{:S(2)}) copy-start(bf16[32,1,8,128]{3,0,2,1:T(8,128)(2,1)S(1)} %collective-permute-done.4) | copy-start | bytes 196612
  39.6 25.6 %collective-permute-start.7 = (bf16[32,10,1,128]{3,0,2,1:T(8,128)(2,1)}, bf16[32,10,1,128]{3,0,2,1:T(8,128)(2,1)}, u32[]{:S(2)}, u32[]{:S(2)}) collective-permute-start(bf16[32,10,1,128]{3,0,2,1:T(8,128)(2,1)} %get-tuple-element.44), channel_id=1, source_target_pairs={{1,0},{2,1},{3,2},{5,4},{6,5},{7,6},{9,8},{10,9},{11,10},{13,12},{... | collective-permute-start | bytes 245768 | tf_op jit(solution)/shard_map/ppermute | solution.py:17
  40.9 24.3 %collective-permute-start.6 = (bf16[32,10,1,128]{3,0,2,1:T(8,128)(2,1)}, bf16[32,10,1,128]{3,0,2,1:T(8,128)(2,1)}, u32[]{:S(2)}, u32[]{:S(2)}) collective-permute-start(bf16[32,10,1,128]{3,0,2,1:T(8,128)(2,1)} %get-tuple-element.43), channel_id=1, source_target_pairs={{0,1},{1,2},{2,3},{4,5},{5,6},{6,7},{8,9},{9,10},{10,11},{12,13},{... | collective-permute-start | bytes 245768 | tf_op jit(solution)/shard_map/ppermute | solution.py:16
  60.3 4.0 %copy-start.36 = (bf16[32,1,1,3,32]{4,0,3,2,1:T(8,128)(2,1)S(1)}, bf16[32,1,1,3,32]{4,0,3,2,1:T(8,128)(2,1)}, u32[]{:S(2)}) copy-start(bf16[32,1,1,3,32]{4,0,3,2,1:T(8,128)(2,1)} %get-tuple-element.74) | copy-start | bytes 18436
  60.3 4.1 %copy-start.35 = (bf16[32,1,1,3,32]{4,0,3,2,1:T(8,128)(2,1)S(1)}, bf16[32,1,1,3,32]{4,0,3,2,1:T(8,128)(2,1)}, u32[]{:S(2)}) copy-start(bf16[32,1,1,3,32]{4,0,3,2,1:T(8,128)(2,1)} %get-tuple-element.75) | copy-start | bytes 18436
  60.3 4.2 %copy-start.34 = (bf16[32,1,1,3,32]{4,0,3,2,1:T(8,128)(2,1)S(1)}, bf16[32,1,1,3,32]{4,0,3,2,1:T(8,128)(2,1)}, u32[]{:S(2)}) copy-start(bf16[32,1,1,3,32]{4,0,3,2,1:T(8,128)(2,1)} %get-tuple-element.76) | copy-start | bytes 18436
  60.3 4.3 %copy-start.33 = (bf16[32,1,1,3,32]{4,0,3,2,1:T(8,128)(2,1)S(1)}, bf16[32,1,1,3,32]{4,0,3,2,1:T(8,128)(2,1)}, u32[]{:S(2)}) copy-start(bf16[32,1,1,3,32]{4,0,3,2,1:T(8,128)(2,1)} %get-tuple-element.77) | copy-start | bytes 18436
  60.3 4.4 %copy-start.32 = (bf16[32,1,1,3,32]{4,0,3,2,1:T(8,128)(2,1)S(1)}, bf16[32,1,1,3,32]{4,0,3,2,1:T(8,128)(2,1)}, u32[]{:S(2)}) copy-start(bf16[32,1,1,3,32]{4,0,3,2,1:T(8,128)(2,1)} %get-tuple-element.78) | copy-start | bytes 18436
  60.3 4.5 %copy-start.31 = (bf16[32,1,1,3,32]{4,0,3,2,1:T(8,128)(2,1)S(1)}, bf16[32,1,1,3,32]{4,0,3,2,1:T(8,128)(2,1)}, u32[]{:S(2)}) copy-start(bf16[32,1,1,3,32]{4,0,3,2,1:T(8,128)(2,1)} %get-tuple-element.79) | copy-start | bytes 18436
  60.3 4.6 %copy-start.30 = (bf16[32,1,1,3,32]{4,0,3,2,1:T(8,128)(2,1)S(1)}, bf16[32,1,1,3,32]{4,0,3,2,1:T(8,128)(2,1)}, u32[]{:S(2)}) copy-start(bf16[32,1,1,3,32]{4,0,3,2,1:T(8,128)(2,1)} %get-tuple-element.80) | copy-start | bytes 18436
  60.4 4.7 %copy-start.29 = (bf16[32,1,1,3,32]{4,0,3,2,1:T(8,128)(2,1)S(1)}, bf16[32,1,1,3,32]{4,0,3,2,1:T(8,128)(2,1)}, u32[]{:S(2)}) copy-start(bf16[32,1,1,3,32]{4,0,3,2,1:T(8,128)(2,1)} %get-tuple-element.73) | copy-start | bytes 18436
  60.4 4.8 %copy-start.7 = (bf16[32,1,8,128]{3,0,2,1:T(8,128)(2,1)S(1)}, bf16[32,1,8,128]{3,0,2,1:T(8,128)(2,1)}, u32[]{:S(2)}) copy-start(bf16[32,1,8,128]{3,0,2,1:T(8,128)(2,1)} %copy-done.6) | copy-start | bytes 196612
  60.4 4.8 %copy-start.9 = (bf16[32,1,8,128]{3,0,2,1:T(8,128)(2,1)S(1)}, bf16[32,1,8,128]{3,0,2,1:T(8,128)(2,1)}, u32[]{:S(2)}) copy-start(bf16[32,1,8,128]{3,0,2,1:T(8,128)(2,1)} %copy-done.8) | copy-start | bytes 196612
  83.0 11.2 %collective-permute-start.9 = (bf16[32,1,8,128]{3,0,2,1:T(8,128)(2,1)}, bf16[32,1,8,128]{3,0,2,1:T(8,128)(2,1)S(1)}, u32[]{:S(2)}, u32[]{:S(2)}) collective-permute-start(bf16[32,1,8,128]{3,0,2,1:T(8,128)(2,1)} %get-tuple-element.50), channel_id=1, source_target_pairs={{4,0},{8,4},{12,8},{16,12},{20,16},{24,20},{28,24},{5,1},{9,5},{13... | collective-permute-start | bytes 196616 | tf_op jit(solution)/shard_map/ppermute | solution.py:17
  84.3 9.9 %collective-permute-start.8 = (bf16[32,1,8,128]{3,0,2,1:T(8,128)(2,1)}, bf16[32,1,8,128]{3,0,2,1:T(8,128)(2,1)S(1)}, u32[]{:S(2)}, u32[]{:S(2)}) collective-permute-start(bf16[32,1,8,128]{3,0,2,1:T(8,128)(2,1)} %get-tuple-element.49), channel_id=1, source_target_pairs={{0,4},{4,8},{8,12},{12,16},{16,20},{20,24},{24,28},{1,5},{5,9},{9,... | collective-permute-start | bytes 196616 | tf_op jit(solution)/shard_map/ppermute | solution.py:16
  94.2 8.0 %collective-permute-start.11 = (bf16[32,10,1,128]{3,0,2,1:T(8,128)(2,1)S(1)}, bf16[32,10,1,128]{3,0,2,1:T(8,128)(2,1)S(1)}, u32[]{:S(2)}, u32[]{:S(2)}) collective-permute-start(bf16[32,10,1,128]{3,0,2,1:T(8,128)(2,1)S(1)} %get-tuple-element.42), channel_id=1, source_target_pairs={{1,0},{2,1},{3,2},{5,4},{6,5},{7,6},{9,8},{10,9},{11,10},{13,12},{... | collective-permute-start | bytes 245768 | tf_op jit(solution)/shard_map/ppermute | solution.py:17
  95.8 7.5 %collective-permute-start.10 = (bf16[32,10,1,128]{3,0,2,1:T(8,128)(2,1)S(1)}, bf16[32,10,1,128]{3,0,2,1:T(8,128)(2,1)S(1)}, u32[]{:S(2)}, u32[]{:S(2)}) collective-permute-start(bf16[32,10,1,128]{3,0,2,1:T(8,128)(2,1)S(1)} %get-tuple-element.41), channel_id=1, source_target_pairs={{0,1},{1,2},{2,3},{4,5},{5,6},{6,7},{8,9},{9,10},{10,11},{12,13},{... | collective-permute-start | bytes 245768 | tf_op jit(solution)/shard_map/ppermute | solution.py:16
  115.5 7.8 %copy-start.41 = (f32[32]{0:T(128)S(1)}, f32[32]{0:T(128)}, u32[]{:S(2)}) copy-start(f32[32]{0:T(128)} %get-tuple-element.91) | copy-start | bytes 388
  116.8 52.9 %collective-permute-start.13 = (bf16[32,1,8,128]{3,0,2,1:T(8,128)(2,1)S(1)}, bf16[32,1,8,128]{3,0,2,1:T(8,128)(2,1)S(1)}, u32[]{:S(2)}, u32[]{:S(2)}) collective-permute-start(bf16[32,1,8,128]{3,0,2,1:T(8,128)(2,1)S(1)} %get-tuple-element.48), channel_id=1, source_target_pairs={{4,0},{8,4},{12,8},{16,12},{20,16},{24,20},{28,24},{5,1},{9,5},{13... | collective-permute-start | bytes 196616 | tf_op jit(solution)/shard_map/ppermute | solution.py:17
  118.1 51.6 %collective-permute-start.12 = (bf16[32,1,8,128]{3,0,2,1:T(8,128)(2,1)S(1)}, bf16[32,1,8,128]{3,0,2,1:T(8,128)(2,1)S(1)}, u32[]{:S(2)}, u32[]{:S(2)}) collective-permute-start(bf16[32,1,8,128]{3,0,2,1:T(8,128)(2,1)S(1)} %get-tuple-element.47), channel_id=1, source_target_pairs={{0,4},{4,8},{8,12},{12,16},{16,20},{20,24},{24,28},{1,5},{5,9},{9,... | collective-permute-start | bytes 196616 | tf_op jit(solution)/shard_map/ppermute | solution.py:16
  169.7 136.0 %collective-permute-start.15 = (bf16[32,10,1,128]{3,0,2,1:T(8,128)(2,1)S(1)}, bf16[32,10,1,128]{3,0,2,1:T(8,128)(2,1)S(1)}, u32[]{:S(2)}, u32[]{:S(2)}) collective-permute-start(bf16[32,10,1,128]{3,0,2,1:T(8,128)(2,1)S(1)} %get-tuple-element.40), channel_id=1, source_target_pairs={{1,0},{2,1},{3,2},{5,4},{6,5},{7,6},{9,8},{10,9},{11,10},{13,12},{... | collective-permute-start | bytes 245768 | tf_op jit(solution)/shard_map/ppermute | solution.py:17
  171.0 134.7 %collective-permute-start.14 = (bf16[32,10,1,128]{3,0,2,1:T(8,128)(2,1)S(1)}, bf16[32,10,1,128]{3,0,2,1:T(8,128)(2,1)S(1)}, u32[]{:S(2)}, u32[]{:S(2)}) collective-permute-start(bf16[32,10,1,128]{3,0,2,1:T(8,128)(2,1)S(1)} %get-tuple-element.39), channel_id=1, source_target_pairs={{0,1},{1,2},{2,3},{4,5},{5,6},{6,7},{8,9},{9,10},{10,11},{12,13},{... | collective-permute-start | bytes 245768 | tf_op jit(solution)/shard_map/ppermute | solution.py:16
  (27 other events, 29.4 us)
Sparse Core Ops, SparseCore 0:
  169.8 131.8 all-reduce.8
where the time goes:
time: 322 us; the launch traced here: 321 us
  waiting for transfers between devices  130 us (40%)
  starting transfers between devices  47.6 us (15%)
  blocking collectives  44.2 us (14%)
  local copies, waits for them, and re-layouts  34.7 us (11%)
  matrix products  29.3 us (9%)
  other arithmetic  19.9 us (6%)
  between operations  15.2 us (5%)
    psum x1, waiting for transfers between devices, body(): lax.psum((local_w_one, local_b_one, local_w_two, local_b_two), ('gx', 'gy'))  126 us
    psum x1, blocking collectives, body(): lax.psum((local_w_one, local_b_one, local_w_two, local_b_two), ('gx', 'gy'))  44.2 us
    ppermute x8, starting transfers between devices, padded_2(): before = lax.ppermute(last, axis, up)  37 us
    dot_general x36, matrix products, convolve(): jnp.einsum('ok,kxyz->oxyz', kernel, window, preferred_element_type=jnp.fl...  15.9 us
    dot_general x18, matrix products, weight_grad(): jnp.einsum('oxyz,kxyz->ok', upstream, window, preferred_element_type=jnp....  13.4 us
    ppermute x8, starting transfers between devices, padded_2(): after = lax.ppermute(first, axis, down)  10.6 us
    reshape x2, local copies, waits for them, and re-layouts, expand(): jnp.repeat(jnp.repeat(jnp.repeat(field, factor, axis=-3), factor, axis=-2...  7.38 us
    concatenate x4, other arithmetic, padded_2(): x = jnp.concatenate([before, x, after], axis=dim)  6.95 us
  transfers between devices with their start and end apart: 17, of which 5 were waited for; matrix products, arithmetic and copies ran while one was open for 11% of the time, Pallas kernels for 0%

commit v1 on v0

v1 whole, which is shorter than its diff:
```python
import functools
import math

import jax
import jax.numpy as jnp
import numpy as np
from jax import lax
from jax.experimental import pallas as pl
from jax.experimental.pallas import tpu as pltpu
from jax.sharding import PartitionSpec as P

MESH = pl.DeviceIdType.MESH
HALO = 4
SIDES = tuple((sx, sy) for sx in (-1, 0, 1) for sy in (-1, 0, 1) if (sx, sy) != (0, 0))
BF = jnp.bfloat16
F32 = jnp.float32


def edge(side, cells, width):
    if side == 0:
        return 0, cells
    return (0, width) if side < 0 else (cells - width, width)


def landing(side, cells, width):
    if side == 0:
        return width, cells
    return (width + cells, width) if side < 0 else (0, width)


def exchange_kernel(nx, ny, depth, own_f, own_p, out_f, out_p, send_sem, recv_sem, local_sem):
    gx = lax.axis_index("gx")
    gy = lax.axis_index("gy")
    pairs = ((own_f, out_f, HALO), (own_p, out_p, 1))

    def exists(sx, sy):
        ok_x = jnp.logical_and(gx + sx >= 0, gx + sx < nx)
        ok_y = jnp.logical_and(gy + sy >= 0, gy + sy < ny)
        return jnp.logical_and(ok_x, ok_y)

    barrier = pltpu.get_barrier_semaphore()
    for sx, sy in SIDES:
        @pl.when(exists(sx, sy))
        def _():
            pl.semaphore_signal(barrier, inc=1, device_id=(gx + sx, gy + sy), device_id_type=MESH)
    locals_ = []
    for n, (own, out, width) in enumerate(pairs):
        cx, cy = own.shape[0], own.shape[2] // depth
        locals_.append(
            pltpu.make_async_copy(
                own, out.at[width : width + cx, :, width * depth : (width + cy) * depth], local_sem.at[n]
            )
        )
    for copy in locals_:
        copy.start()
    span_x = 1 + (gx > 0).astype(jnp.int32) + (gx < nx - 1).astype(jnp.int32)
    span_y = 1 + (gy > 0).astype(jnp.int32) + (gy < ny - 1).astype(jnp.int32)
    pl.semaphore_wait(barrier, span_x * span_y - 1)

    def copy_of(n, k):
        own, out, width = pairs[n]
        sx, sy = SIDES[k]
        cx, cy = own.shape[0], own.shape[2] // depth
        fx, lx = edge(sx, cx, width)
        fy, ly = edge(sy, cy, width)
        tx, _ = landing(sx, cx, width)
        ty, _ = landing(sy, cy, width)
        return pltpu.make_async_remote_copy(
            src_ref=own.at[fx : fx + lx, :, fy * depth : (fy + ly) * depth],
            dst_ref=out.at[tx : tx + lx, :, ty * depth : (ty + ly) * depth],
            send_sem=send_sem.at[n, k],
            recv_sem=recv_sem.at[n, k],
            device_id=(gx + sx, gy + sy),
            device_id_type=MESH,
        )

    for k, (sx, sy) in enumerate(SIDES):
        @pl.when(exists(sx, sy))
        def _():
            for n in range(2):
                copy_of(n, k).start()
    for copy in locals_:
        copy.wait()
    for k, (sx, sy) in enumerate(SIDES):
        @pl.when(exists(sx, sy))
        def _():
            for n in range(2):
                copy_of(n, k).wait_send()

        @pl.when(exists(-sx, -sy))
        def _():
            for n in range(2):
                copy_of(n, k).wait_recv()


def compute_kernel(
    cx, cy, depth, chans,
    f_ref, p_ref, mz_ref, w1_ref, w2_ref, w2b_ref, w1b_ref, b1_ref, b2_ref,
    gin_ref, gw_ref, s1, s2, s3, s4, bias_acc,
):
    lane = lax.broadcasted_iota(jnp.int32, (1, depth), 1)
    not_first = lane != 0
    not_last = lane != depth - 1
    lane_odd = lane % 2

    def mask_row(x, first, count):
        bx = (x + 8 - HALO) // 8
        flags = mz_ref[bx]
        parts = []
        for y in range(first, first + count):
            by = (y + 8 - HALO) // 8
            parts.append(flags[by : by + 1, :])
        return jnp.concatenate(parts, axis=1)

    def put(stack, x, value):
        count = value.shape[1] // depth
        rounded = value.astype(BF)
        wide = rounded.astype(F32)
        before, after = [], []
        for y in range(count):
            tile = wide[:, y * depth : (y + 1) * depth]
            before.append(jnp.where(not_first, pltpu.roll(tile, 1, 1), 0.0))
            after.append(jnp.where(not_last, pltpu.roll(tile, depth - 1, 1), 0.0))
        stack[x, 0:chans, :] = jnp.concatenate(before, axis=1).astype(BF)
        stack[x, chans : 2 * chans, :] = rounded
        stack[x, 2 * chans : 3 * chans, :] = jnp.concatenate(after, axis=1).astype(BF)

    def conv(weight, stack, x):
        width = stack.shape[2]
        rows = stack[pl.ds(x, 3)].reshape(9 * chans, width)
        full = jnp.dot(weight[...], rows, preferred_element_type=F32)
        keep = width - 2 * depth
        total = full[0:chans, 0:keep]
        total += full[chans : 2 * chans, depth : depth + keep]
        total += full[2 * chans : 3 * chans, 2 * depth : 2 * depth + keep]
        return total

    def grad(slot, delta, stack, x, first):
        width = (cy + 2) * depth
        rows = stack[pl.ds(x, 3), :, first * depth : first * depth + width].reshape(9 * chans, width)
        shifted = []
        for b in range(3):
            parts = []
            if b:
                parts.append(jnp.zeros((chans, b * depth), BF))
            parts.append(delta)
            if b < 2:
                parts.append(jnp.zeros((chans, (2 - b) * depth), BF))
            shifted.append(jnp.concatenate(parts, axis=1))
        left = jnp.concatenate(shifted, axis=0)
        gw_ref[slot, :, 0 : 9 * chans] += lax.dot_general(
            left, rows, (((1,), (1,)), ((), ())), preferred_element_type=F32
        )
        bias_acc[slot] += delta.astype(F32)

    gw_ref[...] = jnp.zeros_like(gw_ref)
    bias_acc[...] = jnp.zeros_like(bias_acc)

    @pl.loop(0, cx + 8)
    def _(x):
        mask = mask_row(x, 0, cy + 8)
        put(s1, x, jnp.where(mask > 0, f_ref[x].astype(F32), 0.0))

    @pl.loop(0, cx + 6)
    def _(x):
        mask = mask_row(x + 1, 1, cy + 6)
        pre = conv(w1_ref, s1, x) + b1_ref[...]
        put(s2, x, jnp.where(mask > 0, jnp.maximum(pre, 0.0), 0.0))

    @pl.loop(0, cx + 4)
    def _(x):
        mask = mask_row(x + 2, 2, cy + 4)
        pre = conv(w2_ref, s2, x) + b2_ref[...]
        pooled = p_ref[x // 2].astype(F32)
        vals, hits = [], []
        for y in range(cy + 4):
            half = y // 2
            code = (4 * (x % 2) + 2 * (y % 2) + lane_odd).astype(F32)
            vals.append(pooled[0:chans, half * depth : (half + 1) * depth])
            hits.append(
                jnp.where(pooled[chans : 2 * chans, half * depth : (half + 1) * depth] == code, 1.0, 0.0)
            )
        up = jnp.concatenate(vals, axis=1)
        hit = jnp.concatenate(hits, axis=1) * mask
        chosen = jnp.where(pre > 0, hit, 0.0)
        put(s3, x, jnp.where(chosen > 0, up, 0.0))

    @pl.loop(0, cx)
    def _(x):
        delta = s3[x + 2, chans : 2 * chans, 2 * depth : (2 + cy) * depth]
        grad(1, delta, s2, x + 2, 2)

    @pl.loop(0, cx + 2)
    def _(x):
        back = conv(w2b_ref, s3, x)
        hidden = s2[x + 2, chans : 2 * chans, 2 * depth : (4 + cy) * depth].astype(F32)
        put(s4, x, jnp.where(hidden > 0, back, 0.0))

    @pl.loop(0, cx)
    def _(x):
        delta = s4[x + 1, chans : 2 * chans, depth : (1 + cy) * depth]
        grad(0, delta, s1, x + 3, 3)

    @pl.loop(0, cx)
    def _(x):
        mask = mask_row(x + 4, 4, cy)
        back = conv(w1b_ref, s4, x)
        gin_ref[x] = jnp.where(mask > 0, back, 0.0).astype(BF)

    for slot in range(2):
        total = jnp.sum(bias_acc[slot], axis=1, keepdims=True)
        gw_ref[slot, 0:chans, 9 * chans :] = jnp.broadcast_to(
            total, (chans, gw_ref.shape[2] - 9 * chans)
        )


def sum_kernel(nx, ny, g_ref, o_ref, r1, h, r2, s1, q1, s2, q2, s3, q3, s4, q4):
    gx = lax.axis_index("gx")
    gy = lax.axis_index("gy")

    def peer_x(k):
        return lax.rem(gx + k, nx)

    def peer_y(k):
        return lax.rem(gy + k, ny)

    barrier = pltpu.get_barrier_semaphore()
    for k in range(1, ny):
        pl.semaphore_signal(barrier, inc=1, device_id=(gx, peer_y(k)), device_id_type=MESH)
    for k in range(1, nx):
        pl.semaphore_signal(barrier, inc=1, device_id=(peer_x(k), gy), device_id_type=MESH)
    pl.semaphore_wait(barrier, nx + ny - 2)

    def remote(src, dst, ss, rs, k, device):
        return pltpu.make_async_remote_copy(
            src_ref=src, dst_ref=dst, send_sem=ss.at[k], recv_sem=rs.at[k],
            device_id=device, device_id_type=MESH,
        )

    def run(copies):
        for c in copies:
            c.start()
        for c in copies:
            c.wait_send()
        for c in copies:
            c.wait_recv()

    run([remote(g_ref.at[peer_y(k)], r1.at[k], s1, q1, k, (gx, peer_y(k))) for k in range(1, ny)])
    part = g_ref[gy].astype(F32)
    for k in range(1, ny):
        part += r1[k].astype(F32)
    h[...] = part.astype(BF)
    run([remote(h.at[peer_x(k)], r2.at[k], s2, q2, k, (peer_x(k), gy)) for k in range(1, nx)])
    full = h[gx].astype(F32)
    for k in range(1, nx):
        full += r2[k].astype(F32)
    o_ref[gy, gx] = full.astype(BF)
    run([
        remote(o_ref.at[gy, gx], o_ref.at[gy, gx], s3, q3, k, (peer_x(k), gy)) for k in range(1, nx)
    ])
    run([remote(o_ref.at[gy], o_ref.at[gy], s4, q4, k, (gx, peer_y(k))) for k in range(1, ny)])


def rows_of(weight):
    channels = weight.shape[0]
    return weight.transpose(2, 0, 1, 3, 4).reshape(3 * channels, -1)


def flipped(weight):
    return jnp.flip(weight, (1, 2, 3)).transpose(4, 1, 2, 3, 0)


def vmem(count):
    return [pl.BlockSpec(memory_space=pltpu.VMEM)] * count


def body(features, occupancy, weight_one, bias_one, weight_two, bias_two, grad_pooled, pool_choice):
    chans, cx, cy, depth = features.shape
    nx, ny = lax.axis_size("gx"), lax.axis_size("gy")
    brick_x, brick_y = cx // 8, cy // 8
    padded_flags = jnp.pad(occupancy, ((1, 1), (1, 1), (0, 0)))
    flags = lax.dynamic_slice(
        padded_flags,
        (lax.axis_index("gx") * brick_x, lax.axis_index("gy") * brick_y, jnp.int32(0)),
        (brick_x + 2, brick_y + 2, occupancy.shape[2]),
    )
    mz = jnp.repeat(flags, 8, axis=2).astype(F32)
    own_f = features.transpose(1, 0, 2, 3).reshape(cx, chans, cy * depth)
    spread = np.repeat(np.eye(depth // 2, dtype=np.float32), 2, axis=1)
    both = jnp.concatenate([grad_pooled, pool_choice.astype(BF)], axis=0)
    both = both.transpose(1, 0, 2, 3)
    both = jnp.dot(both, jnp.asarray(spread, BF), preferred_element_type=F32).astype(BF)
    own_p = both.reshape(cx // 2, 2 * chans, (cy // 2) * depth)

    shapes = (
        jax.ShapeDtypeStruct((cx + 2 * HALO, chans, (cy + 2 * HALO) * depth), BF),
        jax.ShapeDtypeStruct((cx // 2 + 2, 2 * chans, (cy // 2 + 2) * depth), BF),
    )
    wide_f, wide_p = pl.pallas_call(
        functools.partial(exchange_kernel, nx, ny, depth),
        out_shape=shapes,
        in_specs=vmem(2),
        out_specs=tuple(vmem(2)),
        scratch_shapes=[
            pltpu.SemaphoreType.DMA((2, 8)),
            pltpu.SemaphoreType.DMA((2, 8)),
            pltpu.SemaphoreType.DMA((2,)),
        ],
        compiler_params=pltpu.CompilerParams(collective_id=0, has_side_effects=True),
        name="exchange",
    )(own_f, own_p)

    lanes = -(-(9 * chans + 1) // 128) * 128
    gin, gw = pl.pallas_call(
        functools.partial(compute_kernel, cx, cy, depth, chans),
        out_shape=(
            jax.ShapeDtypeStruct((cx, chans, cy * depth), BF),
            jax.ShapeDtypeStruct((2, 3 * chans, lanes), F32),
        ),
        in_specs=vmem(9),
        out_specs=tuple(vmem(2)),
        scratch_shapes=[
            pltpu.VMEM((cx + 8, 3 * chans, (cy + 8) * depth), BF),
            pltpu.VMEM((cx + 6, 3 * chans, (cy + 6) * depth), BF),
            pltpu.VMEM((cx + 4, 3 * chans, (cy + 4) * depth), BF),
            pltpu.VMEM((cx + 2, 3 * chans, (cy + 2) * depth), BF),
            pltpu.VMEM((2, chans, cy * depth), F32),
        ],
        compiler_params=pltpu.CompilerParams(vmem_limit_bytes=48 * 2**20),
        name="compute",
    )(
        wide_f, wide_p, mz,
        rows_of(weight_one), rows_of(weight_two),
        rows_of(flipped(weight_two)), rows_of(flipped(weight_one)),
        bias_one[:, None], bias_two[:, None],
    )

    rows = 6 * chans
    each = -(-rows // (nx * ny))
    flat = gw.reshape(rows, lanes).astype(BF)
    flat = jnp.pad(flat, ((0, each * nx * ny - rows), (0, 0)))
    summed = pl.pallas_call(
        functools.partial(sum_kernel, nx, ny),
        out_shape=jax.ShapeDtypeStruct((ny, nx, each, lanes), BF),
        in_specs=vmem(1),
        out_specs=vmem(1)[0],
        scratch_shapes=[
            pltpu.VMEM((ny, nx, each, lanes), BF),
            pltpu.VMEM((nx, each, lanes), BF),
            pltpu.VMEM((nx, each, lanes), BF),
        ]
        + [pltpu.SemaphoreType.DMA((n,)) for n in (ny, ny, nx, nx, nx, nx, ny, ny)],
        compiler_params=pltpu.CompilerParams(collective_id=1, has_side_effects=True),
        name="total",
    )(flat.reshape(ny, nx, each, lanes))
    total_cells = cx * nx * cy * ny * depth
    scale = 1.0 / math.sqrt(total_cells)
    sums = summed.reshape(-1, lanes)[:rows].astype(F32) * scale
    sums = sums.reshape(2, 3 * chans, lanes)
    grads = sums[:, :, : 9 * chans].reshape(2, 3, chans, 3, 3, chans).transpose(0, 2, 3, 1, 4, 5)
    biases = sums[:, :chans, 9 * chans]
    grad_input = gin.reshape(cx, chans, cy, depth).transpose(1, 0, 2, 3)
    return grad_input, grads[0], biases[0], grads[1], biases[1]


def solution(mesh):
    placed = (
        P(None, "gx", "gy", None),
        P(),
        P(),
        P(),
        P(),
        P(),
        P(None, "gx", "gy", None),
        P(None, "gx", "gy", None),
    )
    return jax.shard_map(
        body,
        mesh=mesh,
        in_specs=placed,
        out_specs=(P(None, "gx", "gy", None), P(), P(), P(), P()),
        check_vma=False,
    )
```

time: 322 us -> 103 us (0.32)
  waiting for transfers between devices: 130 us -> 0 us
  Pallas kernels: 0 us -> 84.6 us
  starting transfers between devices: 47.6 us -> 0 us
  blocking collectives: 44.2 us -> 0 us
  matrix products: 29.3 us -> 0.97 us
  local copies, waits for them, and re-layouts: 34.7 us -> 13.7 us
  other arithmetic: 19.9 us -> 2.77 us
  between operations: 15.2 us -> 0.81 us
    psum x1 -> x0, waiting for transfers between devices: 126 us -> none  [body(): lax.psum((local_w_one, local_b_one, local_w_two, local_b_two), ('gx', 'gy'))]
    pallas_call x0 -> x3, Pallas kernels: none -> 84.6 us  [the longest x1 37.4 us: body(): pl.pallas_call(functools.partial(sum_kernel, nx, ny), out_shape=jax.Shape...]
    ppermute x16 -> x0, starting transfers between devices: 47.5 us -> none  [the longest x8 37 us: padded_2(): before = lax.ppermute(last, axis, up)]
    psum x1 -> x0, blocking collectives: 44.2 us -> none  [body(): lax.psum((local_w_one, local_b_one, local_w_two, local_b_two), ('gx', 'gy'))]
    dot_general x54 -> x1, matrix products: 29.3 us -> 0.97 us  [body(): jnp.dot(both, jnp.asarray(spread, BF), preferred_element_type=F32)]
    concatenate x8 -> x0, other arithmetic: 10.4 us -> none  [the longest x4 6.95 us: padded_2(): x = jnp.concatenate([before, x, after], axis=dim)]
    another operation x36 -> x4, local copies, waits for them, and re-layouts: 7.23 us -> 0.41 us  [rows_of(): return weight.transpose(2, 0, 1, 3, 4).reshape(3 * channels, -1)]
    broadcast_in_dim x7 -> x3, local copies, waits for them, and re-layouts: 6.28 us -> 1.55 us  [the longest x1 0.74 us: body(): bias_one[:, None]]
  transfers between devices with their start and end apart: 17 -> 0, of which waited for: 5 -> 0; matrix products, arithmetic and copies ran while one was open for 11% -> 0% of each run, Pallas kernels for 0% -> 0%
where the time goes in v1:
time: 103 us
  Pallas kernels  84.6 us (82%)
  local copies, waits for them, and re-layouts  13.7 us (13%)
  other arithmetic  2.77 us (3%)
    pallas_call x1, Pallas kernels, body(): pl.pallas_call(functools.partial(sum_kernel, nx, ny), out_shape=jax.Shape...  37.4 us
    pallas_call x1, Pallas kernels, body(): pl.pallas_call(functools.partial(compute_kernel, cx, cy, depth, chans), o...  28.5 us
    pallas_call x1, Pallas kernels, body(): pl.pallas_call(functools.partial(exchange_kernel, nx, ny, depth), out_sha...  18.7 us
    unnamed x14, local copies, waits for them, and re-layouts  5.48 us

profile of v1, /device:TPU:0, one launch (start us, length us, event | category | flops | bytes accessed | tf_op | source)
XLA Modules:
  0.0 102.9 jit_solution(17555595779007529315)
XLA Ops:
  0.6 0.8 fusion.3
  1.4 0.7 copy.48.b1_ref
  2.1 0.7 copy.49.b2_ref
  2.9 0.1 convert_element_type.26.mz_ref
  3.1 0.9 copy.42
  4.0 1.0 %copy_convert_fusion = bf16[32,4,4,64]{3,0,2,1:T(8,128)(2,1)S(1)} fusion(s32[32,4,4,64]{3,2,1,0:T(4,128)} %param.16), kind=kLoop, calls=%fused_computation.10 | loop fusion | flops 32768 | bytes 196608 | tf_op jit(solution)/shard_map/convert_element_type | solution.py:290
  5.1 1.0 fusion
  6.0 0.7 copy.60
  6.8 0.2 copy.47
  7.0 0.2 reshape.55.w1b_ref
  7.2 0.2 copy.46
  7.4 0.2 reshape.54.w2b_ref
  7.6 0.2 copy.45
  7.8 0.2 reshape.53.w2_ref
  8.0 0.2 copy.44
  8.2 0.2 reshape.52.w1_ref
  8.3 0.1 copy-done.4
  8.5 0.2 reshape.59
  8.7 1.1 %copy.54.own_f = bf16[8,32,1024]{2,1,0:T(8,128)(2,1)} copy(bf16[8,32,1024]{2,0,1:T(8,128)(2,1)S(1)} %reshape.59) | data formatting | bytes 1048576 | tf_op jit(solution)/shard_map/reshape | solution.py:288
  9.8 18.7 %exchange.1 = (bf16[16,32,2048]{2,1,0:T(8,128)(2,1)}, bf16[6,64,768]{2,1,0:T(8,128)(2,1)}) custom-call(bf16[8,32,1024]{2,1,0:T(8,128)(2,1)} %copy.54.own_f, bf16[4,64,512]{2,1,0:T(8,128)(2,1)} %bitcast.47), custom_call_target="tpu_custom_call" | custom-call | tf_op jit(solution)/shard_map/exchange/pallas_call | solution.py:299
  28.5 1.6 %copy-done = bf16[16,32,2048]{2,1,0:T(8,128)(2,1)S(1)} copy-done((bf16[16,32,2048]{2,1,0:T(8,128)(2,1)S(1)}, bf16[16,32,2048]{2,1,0:T(8,128)(2,1)}, u32[]{:S(2)}) %copy-start) | copy-done | bytes 2097176
  30.1 1.1 %copy-done.1 = bf16[6,64,768]{2,1,0:T(8,128)(2,1)S(1)} copy-done((bf16[6,64,768]{2,1,0:T(8,128)(2,1)S(1)}, bf16[6,64,768]{2,1,0:T(8,128)(2,1)}, u32[]{:S(2)}) %copy-start.1) | copy-done | bytes 589848
  31.1 28.5 %compute.1 = (bf16[8,32,1024]{2,1,0:T(8,128)(2,1)S(1)}, f32[2,96,384]{2,1,0:T(8,128)S(1)}) custom-call(bf16[16,32,2048]{2,1,0:T(8,128)(2,1)S(1)} %copy-done, bf16[6,64,768]{2,1,0:T(8,128)(2,1)S(1)} %copy-done.1, f32[3,3,128]{2,1,0:T(4,128)S(1)} %convert_element_type.26.mz_ref, bf16[96,288]{1,0:T(8,128)(2,1)S(1)} %reshape.52.w1_ref, ...), custom_call_target="tpu_custom_call" | custom-call | tf_op jit(solution)/shard_map/compute/pallas_call | solution.py:314
  59.8 0.9 copy_bitcast_fusion
  60.8 0.7 convert_element_type.28.g_ref
  61.5 37.4 %total.1 = bf16[4,8,6,384]{3,2,1,0:T(8,128)(2,1)} custom-call(bf16[4,8,6,384]{3,2,1,0:T(8,128)(2,1)} %convert_element_type.28.g_ref), custom_call_target="tpu_custom_call" | custom-call | tf_op jit(solution)/shard_map/total/pallas_call | solution.py:342
  98.9 1.0 convert_multiply_fusion
  99.9 0.7 slice_reduce_fusion
  100.6 0.5 reshape.57
  101.1 0.2 slice_bitcast_fusion
  101.3 0.8 copy.52
  102.1 0.8 copy.51
  (13 shorter events, 0.3 us)
Async XLA Ops:
  0.6 6.2 %copy-start.3 = (bf16[32,3,3,3,32]{4,0,3,2,1:T(8,128)(2,1)S(1)}, bf16[32,3,3,3,32]{4,0,3,2,1:T(8,128)(2,1)}, u32[]{:S(2)}) copy-start(bf16[32,3,3,3,32]{4,0,3,2,1:T(8,128)(2,1)} %param.11) | copy-start | bytes 165892
  5.1 2.1 %copy-start.2 = (bf16[32,3,3,3,32]{4,0,3,2,1:T(8,128)(2,1)S(1)}, bf16[32,3,3,3,32]{4,0,3,2,1:T(8,128)(2,1)}, u32[]{:S(2)}) copy-start(bf16[32,3,3,3,32]{4,0,3,2,1:T(8,128)(2,1)} %param.13) | copy-start | bytes 165892
  7.4 1.0 %copy-start.4 = (bf16[32,8,8,128]{3,2,1,0:T(8,128)(2,1)S(1)}, bf16[32,8,8,128]{3,2,1,0:T(8,128)(2,1)}, u32[]{:S(2)}) copy-start(bf16[32,8,8,128]{3,2,1,0:T(8,128)(2,1)} %param.9) | copy-start | bytes 1572868
  28.5 1.6 %copy-start = (bf16[16,32,2048]{2,1,0:T(8,128)(2,1)S(1)}, bf16[16,32,2048]{2,1,0:T(8,128)(2,1)}, u32[]{:S(2)}) copy-start(bf16[16,32,2048]{2,1,0:T(8,128)(2,1)} %get-tuple-element.9.f_ref) | copy-start | bytes 6291460
  30.1 1.1 %copy-start.1 = (bf16[6,64,768]{2,1,0:T(8,128)(2,1)S(1)}, bf16[6,64,768]{2,1,0:T(8,128)(2,1)}, u32[]{:S(2)}) copy-start(bf16[6,64,768]{2,1,0:T(8,128)(2,1)} %get-tuple-element.10.p_ref) | copy-start | bytes 1769476

commit v2 on v1

--- a/solution.py
+++ b/solution.py
@@ -10,28 +10,32 @@
 from jax.sharding import PartitionSpec as P
 
 MESH = pl.DeviceIdType.MESH
-HALO = 4
+HALO = 2
 SIDES = tuple((sx, sy) for sx in (-1, 0, 1) for sy in (-1, 0, 1) if (sx, sy) != (0, 0))
 BF = jnp.bfloat16
 F32 = jnp.float32
 
 
-def edge(side, cells, width):
+def edge(side, cells):
     if side == 0:
         return 0, cells
-    return (0, width) if side < 0 else (cells - width, width)
-
-
-def landing(side, cells, width):
+    return (0, HALO) if side < 0 else (cells - HALO, HALO)
+
+
+def landing(side, cells):
     if side == 0:
-        return width, cells
-    return (width + cells, width) if side < 0 else (0, width)
-
-
-def exchange_kernel(nx, ny, depth, own_f, own_p, out_f, out_p, send_sem, recv_sem, local_sem):
+        return HALO
+    return HALO + cells if side < 0 else 0
+
+
+def main_kernel(
+    nx, ny, cx, cy, depth, chans,
+    own_f, p_ref, mz_ref, w1_ref, w2_ref, w2b_ref, w1b_ref, b1_ref, b2_ref,
+    gin_ref, gw_ref,
+    wide_f, wide_d, s1, s2, s3, s4, bias_acc, send_sem, recv_sem, local_sem,
+):
     gx = lax.axis_index("gx")
     gy = lax.axis_index("gy")
-    pairs = ((own_f, out_f, HALO), (own_p, out_p, 1))
 
     def exists(sx, sy):
         ok_x = jnp.logical_and(gx + sx >= 0, gx + sx < nx)
@@ -43,30 +47,30 @@
         @pl.when(exists(sx, sy))
         def _():
             pl.semaphore_signal(barrier, inc=1, device_id=(gx + sx, gy + sy), device_id_type=MESH)
-    locals_ = []
-    for n, (own, out, width) in enumerate(pairs):
-        cx, cy = own.shape[0], own.shape[2] // depth
-        locals_.append(
-            pltpu.make_async_copy(
-                own, out.at[width : width + cx, :, width * depth : (width + cy) * depth], local_sem.at[n]
-            )
-        )
-    for copy in locals_:
-        copy.start()
+    inner = pltpu.make_async_copy(
+        own_f,
+        wide_f.at[HALO : HALO + cx, :, HALO * depth : (HALO + cy) * depth],
+        local_sem,
+    )
+    inner.start()
     span_x = 1 + (gx > 0).astype(jnp.int32) + (gx < nx - 1).astype(jnp.int32)
     span_y = 1 + (gy > 0).astype(jnp.int32) + (gy < ny - 1).astype(jnp.int32)
     pl.semaphore_wait(barrier, span_x * span_y - 1)
 
     def copy_of(n, k):
-        own, out, width = pairs[n]
         sx, sy = SIDES[k]
-        cx, cy = own.shape[0], own.shape[2] // depth
-        fx, lx = edge(sx, cx, width)
-        fy, ly = edge(sy, cy, width)
-        tx, _ = landing(sx, cx, width)
-        ty, _ = landing(sy, cy, width)
+        fx, lx = edge(sx, cx)
+        fy, ly = edge(sy, cy)
+        tx, ty = landing(sx, cx), landing(sy, cy)
+        if n == 0:
+            out = wide_f
+            src = own_f.at[fx : fx + lx, :, fy * depth : (fy + ly) * depth]
+        else:
+            out = wide_d
+            fx, fy = fx + HALO, fy + HALO
+            src = wide_d.at[fx : fx + lx, :, fy * depth : (fy + ly) * depth]
         return pltpu.make_async_remote_copy(
-            src_ref=own.at[fx : fx + lx, :, fy * depth : (fy + ly) * depth],
+            src_ref=src,
             dst_ref=out.at[tx : tx + lx, :, ty * depth : (ty + ly) * depth],
             send_sem=send_sem.at[n, k],
             recv_sem=recv_sem.at[n, k],
@@ -74,38 +78,31 @@
             device_id_type=MESH,
         )
 
-    for k, (sx, sy) in enumerate(SIDES):
-        @pl.when(exists(sx, sy))
-        def _():
-            for n in range(2):
+    def send(n):
+        for k, (sx, sy) in enumerate(SIDES):
+            @pl.when(exists(sx, sy))
+            def _():
                 copy_of(n, k).start()
-    for copy in locals_:
-        copy.wait()
-    for k, (sx, sy) in enumerate(SIDES):
-        @pl.when(exists(sx, sy))
-        def _():
-            for n in range(2):
+
+    def finish(n):
+        for k, (sx, sy) in enumerate(SIDES):
+            @pl.when(exists(sx, sy))
+            def _():
                 copy_of(n, k).wait_send()
 
-        @pl.when(exists(-sx, -sy))
-        def _():
-            for n in range(2):
+            @pl.when(exists(-sx, -sy))
+            def _():
                 copy_of(n, k).wait_recv()
 
-
-def compute_kernel(
-    cx, cy, depth, chans,
-    f_ref, p_ref, mz_ref, w1_ref, w2_ref, w2b_ref, w1b_ref, b1_ref, b2_ref,
-    gin_ref, gw_ref, s1, s2, s3, s4, bias_acc,
-):
+    send(0)
+
     lane = lax.broadcasted_iota(jnp.int32, (1, depth), 1)
     not_first = lane != 0
     not_last = lane != depth - 1
     lane_odd = lane % 2
 
     def mask_row(x, first, count):
-        bx = (x + 8 - HALO) // 8
-        flags = mz_ref[bx]
+        flags = mz_ref[(x + 8 - HALO) // 8]
         parts = []
         for y in range(first, first + count):
             by = (y + 8 - HALO) // 8
@@ -155,25 +152,27 @@
 
     gw_ref[...] = jnp.zeros_like(gw_ref)
     bias_acc[...] = jnp.zeros_like(bias_acc)
-
-    @pl.loop(0, cx + 8)
-    def _(x):
-        mask = mask_row(x, 0, cy + 8)
-        put(s1, x, jnp.where(mask > 0, f_ref[x].astype(F32), 0.0))
-
-    @pl.loop(0, cx + 6)
-    def _(x):
-        mask = mask_row(x + 1, 1, cy + 6)
+    inner.wait()
+    finish(0)
+
+    @pl.loop(0, cx + 4)
+    def _(x):
+        mask = mask_row(x, 0, cy + 4)
+        put(s1, x, jnp.where(mask > 0, wide_f[x].astype(F32), 0.0))
+
+    @pl.loop(0, cx + 2)
+    def _(x):
+        mask = mask_row(x + 1, 1, cy + 2)
         pre = conv(w1_ref, s1, x) + b1_ref[...]
         put(s2, x, jnp.where(mask > 0, jnp.maximum(pre, 0.0), 0.0))
 
-    @pl.loop(0, cx + 4)
-    def _(x):
-        mask = mask_row(x + 2, 2, cy + 4)
+    @pl.loop(0, cx)
+    def _(x):
+        mask = mask_row(x + 2, 2, cy)
         pre = conv(w2_ref, s2, x) + b2_ref[...]
         pooled = p_ref[x // 2].astype(F32)
         vals, hits = [], []
-        for y in range(cy + 4):
+        for y in range(cy):
             half = y // 2
             code = (4 * (x % 2) + 2 * (y % 2) + lane_odd).astype(F32)
             vals.append(pooled[0:chans, half * depth : (half + 1) * depth])
@@ -183,27 +182,37 @@
         up = jnp.concatenate(vals, axis=1)
         hit = jnp.concatenate(hits, axis=1) * mask
         chosen = jnp.where(pre > 0, hit, 0.0)
-        put(s3, x, jnp.where(chosen > 0, up, 0.0))
+        delta = jnp.where(chosen > 0, up, 0.0).astype(BF)
+        wide_d[x + HALO, :, HALO * depth : (HALO + cy) * depth] = delta
+
+    send(1)
 
     @pl.loop(0, cx)
     def _(x):
-        delta = s3[x + 2, chans : 2 * chans, 2 * depth : (2 + cy) * depth]
-        grad(1, delta, s2, x + 2, 2)
+        delta = wide_d[x + HALO, :, HALO * depth : (HALO + cy) * depth]
+        grad(1, delta, s2, x, 0)
+
+    finish(1)
+
+    @pl.loop(0, cx + 4)
+    def _(x):
+        mask = mask_row(x, 0, cy + 4)
+        put(s3, x, jnp.where(mask > 0, wide_d[x].astype(F32), 0.0))
 
     @pl.loop(0, cx + 2)
     def _(x):
         back = conv(w2b_ref, s3, x)
-        hidden = s2[x + 2, chans : 2 * chans, 2 * depth : (4 + cy) * depth].astype(F32)
+        hidden = s2[x, chans : 2 * chans, :].astype(F32)
         put(s4, x, jnp.where(hidden > 0, back, 0.0))
 
     @pl.loop(0, cx)
     def _(x):
         delta = s4[x + 1, chans : 2 * chans, depth : (1 + cy) * depth]
-        grad(0, delta, s1, x + 3, 3)
+        grad(0, delta, s1, x + 1, 1)
 
     @pl.loop(0, cx)
     def _(x):
-        mask = mask_row(x + 4, 4, cy)
+        mask = mask_row(x + 2, 2, cy)
         back = conv(w1b_ref, s4, x)
         gin_ref[x] = jnp.where(mask > 0, back, 0.0).astype(BF)
 
@@ -292,27 +301,9 @@
     both = jnp.dot(both, jnp.asarray(spread, BF), preferred_element_type=F32).astype(BF)
     own_p = both.reshape(cx // 2, 2 * chans, (cy // 2) * depth)
 
-    shapes = (
-        jax.ShapeDtypeStruct((cx + 2 * HALO, chans, (cy + 2 * HALO) * depth), BF),
-        jax.ShapeDtypeStruct((cx // 2 + 2, 2 * chans, (cy // 2 + 2) * depth), BF),
-    )
-    wide_f, wide_p = pl.pallas_call(
-        functools.partial(exchange_kernel, nx, ny, depth),
-        out_shape=shapes,
-        in_specs=vmem(2),
-        out_specs=tuple(vmem(2)),
-        scratch_shapes=[
-            pltpu.SemaphoreType.DMA((2, 8)),
-            pltpu.SemaphoreType.DMA((2, 8)),
-            pltpu.SemaphoreType.DMA((2,)),
-        ],
-        compiler_params=pltpu.CompilerParams(collective_id=0, has_side_effects=True),
-        name="exchange",
-    )(own_f, own_p)
-
     lanes = -(-(9 * chans + 1) // 128) * 128
     gin, gw = pl.pallas_call(
-        functools.partial(compute_kernel, cx, cy, depth, chans),
+        functools.partial(main_kernel, nx, ny, cx, cy, depth, chans),
         out_shape=(
             jax.ShapeDtypeStruct((cx, chans, cy * depth), BF),
             jax.ShapeDtypeStruct((2, 3 * chans, lanes), F32),
@@ -320,16 +311,23 @@
         in_specs=vmem(9),
         out_specs=tuple(vmem(2)),
         scratch_shapes=[
-            pltpu.VMEM((cx + 8, 3 * chans, (cy + 8) * depth), BF),
-            pltpu.VMEM((cx + 6, 3 * chans, (cy + 6) * depth), BF),
+            pltpu.VMEM((cx + 4, chans, (cy + 4) * depth), BF),
+            pltpu.VMEM((cx + 4, chans, (cy + 4) * depth), BF),
+            pltpu.VMEM((cx + 4, 3 * chans, (cy + 4) * depth), BF),
+            pltpu.VMEM((cx + 2, 3 * chans, (cy + 2) * depth), BF),
             pltpu.VMEM((cx + 4, 3 * chans, (cy + 4) * depth), BF),
             pltpu.VMEM((cx + 2, 3 * chans, (cy + 2) * depth), BF),
             pltpu.VMEM((2, chans, cy * depth), F32),
+            pltpu.SemaphoreType.DMA((2, 8)),
+            pltpu.SemaphoreType.DMA((2, 8)),
+            pltpu.SemaphoreType.DMA,
         ],
-        compiler_params=pltpu.CompilerParams(vmem_limit_bytes=48 * 2**20),
-        name="compute",
+        compiler_params=pltpu.CompilerParams(
+            collective_id=0, has_side_effects=True, vmem_limit_bytes=48 * 2**20
+        ),
+        name="main",
     )(
-        wide_f, wide_p, mz,
+        own_f, own_p, mz,
         rows_of(weight_one), rows_of(weight_two),
         rows_of(flipped(weight_two)), rows_of(flipped(weight_one)),
         bias_one[:, None], bias_two[:, None],

time: 103 us -> 79 us (0.77)
  Pallas kernels: 84.6 us -> 64.5 us
  local copies, waits for them, and re-layouts: 13.7 us -> 9.6 us
    pallas_call x1, Pallas kernels: 37.4 us -> 26.9 us  [body(): pl.pallas_call(functools.partial(sum_kernel, nx, ny), out_shape=jax.Shape...]
    pallas_call x2 -> x1, Pallas kernels: 47.2 us -> 37.6 us  [body(): pl.pallas_call(functools.partial(main_kernel, nx, ny, cx, cy, depth, chan...]
    unnamed x14 -> x10, local copies, waits for them, and re-layouts: 5.48 us -> 2.82 us
where the time goes in v2:
time: 79 us; the launch traced here: 78.7 us
  Pallas kernels  64.5 us (82%)
  local copies, waits for them, and re-layouts  9.6 us (12%)
  other arithmetic  2.77 us (4%)
  matrix products  0.97 us (1%)
  between operations  0.82 us (1%)
    pallas_call x1, Pallas kernels, body(): pl.pallas_call(functools.partial(main_kernel, nx, ny, cx, cy, depth, chan...  37.6 us
    pallas_call x1, Pallas kernels, body(): pl.pallas_call(functools.partial(sum_kernel, nx, ny), out_shape=jax.Shape...  26.9 us
    unnamed x10, local copies, waits for them, and re-layouts  2.82 us

profile of v2, /device:TPU:0, one launch (start us, length us, event | category | flops | bytes accessed | tf_op | source)
XLA Modules:
  0.0 78.7 jit_solution(10576666646660050363)
XLA Ops:
  0.6 0.8 fusion.3
  1.4 0.7 copy.48.b1_ref
  2.1 0.7 copy.49.b2_ref
  2.9 0.1 broadcast_in_dim.9
  2.9 0.1 convert_element_type.26.mz_ref
  3.1 0.9 %copy.42 = bf16[32,4,4,64]{3,0,2,1:T(8,128)(2,1)S(1)} copy(bf16[32,4,4,64]{3,2,1,0:T(4,128)(2,1)} %param.15) | data formatting | bytes 131072 | tf_op args[6]
  4.0 1.0 %copy_convert_fusion = bf16[32,4,4,64]{3,0,2,1:T(8,128)(2,1)S(1)} fusion(s32[32,4,4,64]{3,2,1,0:T(4,128)} %param.16), kind=kLoop, calls=%fused_computation.10 | loop fusion | flops 32768 | bytes 196608 | tf_op jit(solution)/shard_map/convert_element_type | solution.py:299
  5.1 0.0 copy-start
  5.1 1.0 %fusion = bf16[4,4,8,8,128]{4,3,2,1,0:T(8,128)(2,1)S(1)} fusion(bf16[64,128,1,1]{1,0,3,2:T(8,128)(2,1)} %constant.24, bf16[32,4,4,64]{3,0,2,1:T(8,128)(2,1)S(1)} %copy_convert_fusion, bf16[32,4,4,64]{3,0,2,1:T(8,128)(2,1)S(1)} %copy.42), kind=kOutput, calls=%fused_computation.1 | convolution fusion | flops 17170432 | bytes 409600 | tf_op jit(solution)/shard_map/dot_general | solution.py:301
  6.1 0.2 copy.47
  6.3 0.2 reshape.55.w1b_ref
  6.5 0.2 copy.46
  6.7 0.0 copy-start.2
  6.8 0.2 reshape.54.w2b_ref
  7.0 0.2 copy.45
  7.1 0.2 reshape.53.w2_ref
  7.3 0.2 copy.44
  7.5 0.2 reshape.52.w1_ref
  7.7 0.1 copy-done.2
  7.8 0.2 reshape.59
  8.0 0.3 copy.54.own_f
  8.3 37.6 %main.1 = (bf16[8,32,1024]{2,1,0:T(8,128)(2,1)S(1)}, f32[2,96,384]{2,1,0:T(8,128)S(1)}) custom-call(bf16[8,32,1024]{2,1,0:T(8,128)(2,1)S(1)} %copy.54.own_f, bf16[4,64,512]{2,1,0:T(8,128)(2,1)S(1)} %bitcast.43, f32[3,3,128]{2,1,0:T(4,128)S(1)} %convert_element_type.26.mz_ref, bf16[96,288]{1,0:T(8,128)(2,1)S(1)} %reshape.52.w1_ref, ...), custom_call_target="tpu_custom_call" | custom-call | tf_op jit(solution)/shard_map/main/pallas_call | solution.py:305
  46.0 0.1 copy.56
  46.1 0.9 %copy_bitcast_fusion = bf16[32,8,8,128]{3,2,1,0:T(8,128)(2,1)} fusion(bf16[8,32,8,128]{3,2,1,0:T(8,128)(2,1)S(1)} %bitcast.46), kind=kLoop, calls=%fused_computation.4 | loop fusion | bytes 1048576 | tf_op jit(solution)/shard_map/transpose | solution.py:360
  47.0 0.7 convert_element_type.28.g_ref
  47.8 26.9 %total.1 = bf16[4,8,6,384]{3,2,1,0:T(8,128)(2,1)} custom-call(bf16[4,8,6,384]{3,2,1,0:T(8,128)(2,1)} %convert_element_type.28.g_ref), custom_call_target="tpu_custom_call" | custom-call | tf_op jit(solution)/shard_map/total/pallas_call | solution.py:340
  74.6 1.0 %convert_multiply_fusion = f32[4,8,6,384]{3,2,1,0:T(8,128)S(1)} fusion(bf16[4,8,6,384]{3,2,1,0:T(8,128)(2,1)} %total.1), kind=kLoop, calls=%fused_computation.5 | loop fusion | flops 147456 | bytes 442368 | tf_op jit(solution)/shard_map/mul | solution.py:356
  75.6 0.7 slice_reduce_fusion
  76.3 0.5 reshape.57
  76.8 0.2 slice_bitcast_fusion
  77.0 0.8 %copy.52 = f32[32,3,3,3,32]{4,0,3,2,1:T(8,128)} copy(f32[32,3,3,3,32]{4,3,1,0,2:T(4,128)S(1)} %get-tuple-element.21) | data formatting | bytes 221184
  77.8 0.8 %copy.51 = f32[32,3,3,3,32]{4,0,3,2,1:T(8,128)} copy(f32[32,3,3,3,32]{4,3,1,0,2:T(4,128)S(1)} %get-tuple-element.22) | data formatting | bytes 221184
  (8 shorter events, 0.1 us)
Async XLA Ops:
  0.6 5.5 %copy-start.1 = (bf16[32,3,3,3,32]{4,0,3,2,1:T(8,128)(2,1)S(1)}, bf16[32,3,3,3,32]{4,0,3,2,1:T(8,128)(2,1)}, u32[]{:S(2)}) copy-start(bf16[32,3,3,3,32]{4,0,3,2,1:T(8,128)(2,1)} %param.11) | copy-start | bytes 165892
  5.1 1.5 %copy-start = (bf16[32,3,3,3,32]{4,0,3,2,1:T(8,128)(2,1)S(1)}, bf16[32,3,3,3,32]{4,0,3,2,1:T(8,128)(2,1)}, u32[]{:S(2)}) copy-start(bf16[32,3,3,3,32]{4,0,3,2,1:T(8,128)(2,1)} %param.13) | copy-start | bytes 165892
  6.7 1.0 %copy-start.2 = (bf16[32,8,8,128]{3,2,1,0:T(8,128)(2,1)S(1)}, bf16[32,8,8,128]{3,2,1,0:T(8,128)(2,1)}, u32[]{:S(2)}) copy-start(bf16[32,8,8,128]{3,2,1,0:T(8,128)(2,1)} %param.9) | copy-start | bytes 1572868

commit v3 on v2

v3 whole, which is shorter than its diff:
```python
import functools
import math

import jax
import jax.numpy as jnp
import numpy as np
from jax import lax
from jax.experimental import pallas as pl
from jax.experimental.pallas import tpu as pltpu
from jax.sharding import PartitionSpec as P

MESH = pl.DeviceIdType.MESH
HALO = 2
SIDES = tuple((sx, sy) for sx in (-1, 0, 1) for sy in (-1, 0, 1) if (sx, sy) != (0, 0))
BF = jnp.bfloat16
F32 = jnp.float32


def edge(side, cells):
    if side == 0:
        return 0, cells
    return (0, HALO) if side < 0 else (cells - HALO, HALO)


def landing(side, cells):
    if side == 0:
        return HALO
    return HALO + cells if side < 0 else 0


def main_kernel(
    nx, ny, cx, cy, depth, chans,
    own_f, p_ref, mz_ref, w1_ref, w2_ref, w2b_ref, w1b_ref, b_ref,
    gin_ref, o_ref,
    wide_f, wide_d, s1, s2, s3, s4, bias_acc, gw_ref, g_ref, r1, h, r2,
    send_sem, recv_sem, sum_send_x, sum_recv_x, sum_send_y, sum_recv_y,
):
    gx = lax.axis_index("gx")
    gy = lax.axis_index("gy")

    def exists(sx, sy):
        ok_x = jnp.logical_and(gx + sx >= 0, gx + sx < nx)
        ok_y = jnp.logical_and(gy + sy >= 0, gy + sy < ny)
        return jnp.logical_and(ok_x, ok_y)

    def peer_x(k):
        return lax.rem(gx + k, nx)

    def peer_y(k):
        return lax.rem(gy + k, ny)

    barrier = pltpu.get_barrier_semaphore()
    for k in range(1, ny):
        pl.semaphore_signal(barrier, inc=1, device_id=(gx, peer_y(k)), device_id_type=MESH)
    for k in range(1, nx):
        pl.semaphore_signal(barrier, inc=1, device_id=(peer_x(k), gy), device_id_type=MESH)
    for sx, sy in SIDES:
        if sx and sy:
            @pl.when(exists(sx, sy))
            def _():
                pl.semaphore_signal(
                    barrier, inc=1, device_id=(gx + sx, gy + sy), device_id_type=MESH
                )
    beside_x = (gx > 0).astype(jnp.int32) + (gx < nx - 1).astype(jnp.int32)
    beside_y = (gy > 0).astype(jnp.int32) + (gy < ny - 1).astype(jnp.int32)
    pl.semaphore_wait(barrier, nx + ny - 2 + beside_x * beside_y)

    def copy_of(n, k):
        sx, sy = SIDES[k]
        fx, lx = edge(sx, cx)
        fy, ly = edge(sy, cy)
        tx, ty = landing(sx, cx), landing(sy, cy)
        if n == 0:
            out = wide_f
            src = own_f.at[fx : fx + lx, fy : fy + ly]
        else:
            out = wide_d
            fx, fy = fx + HALO, fy + HALO
            src = wide_d.at[fx : fx + lx, fy : fy + ly]
        return pltpu.make_async_remote_copy(
            src_ref=src,
            dst_ref=out.at[tx : tx + lx, ty : ty + ly],
            send_sem=send_sem.at[n, k],
            recv_sem=recv_sem.at[n, k],
            device_id=(gx + sx, gy + sy),
            device_id_type=MESH,
        )

    def send(n):
        for k, (sx, sy) in enumerate(SIDES):
            @pl.when(exists(sx, sy))
            def _():
                copy_of(n, k).start()

    def finish(n):
        for k, (sx, sy) in enumerate(SIDES):
            @pl.when(exists(sx, sy))
            def _():
                copy_of(n, k).wait_send()

            @pl.when(exists(-sx, -sy))
            def _():
                copy_of(n, k).wait_recv()

    send(0)

    lane = lax.broadcasted_iota(jnp.int32, (1, depth), 1)
    not_first = lane != 0
    not_last = lane != depth - 1
    lane_odd = lane % 2

    def mask_row(x, first, count):
        flags = mz_ref[(x + 8 - HALO) // 8]
        parts = []
        for y in range(first, first + count):
            by = (y + 8 - HALO) // 8
            parts.append(flags[by : by + 1, :])
        return jnp.concatenate(parts, axis=1)

    def put(stack, x, value, first=0):
        count = value.shape[1] // depth
        rounded = value.astype(BF)
        wide = rounded.astype(F32)
        before, after = [], []
        for y in range(count):
            tile = wide[:, y * depth : (y + 1) * depth]
            before.append(jnp.where(not_first, pltpu.roll(tile, 1, 1), 0.0))
            after.append(jnp.where(not_last, pltpu.roll(tile, depth - 1, 1), 0.0))
        where = slice(first * depth, (first + count) * depth)
        stack[x, 0:chans, where] = jnp.concatenate(before, axis=1).astype(BF)
        stack[x, chans : 2 * chans, where] = rounded
        stack[x, 2 * chans : 3 * chans, where] = jnp.concatenate(after, axis=1).astype(BF)

    def tiles(ref, x, first, count):
        return jnp.concatenate([ref[x, y] for y in range(first, first + count)], axis=1)

    def put_cells(stack, ref, x, first, count):
        mask = mask_row(x, first, count)
        put(stack, x, jnp.where(mask > 0, tiles(ref, x, first, count).astype(F32), 0.0), first)

    def put_halo(stack, ref):
        @pl.loop(0, 2 * HALO)
        def _(n):
            put_cells(stack, ref, n + cx * (n // HALO), 0, cy + 2 * HALO)

        @pl.loop(HALO, HALO + cx)
        def _(x):
            put_cells(stack, ref, x, 0, HALO)
            put_cells(stack, ref, x, HALO + cy, HALO)

    def conv(weight, stack, x):
        width = stack.shape[2]
        rows = stack[pl.ds(x, 3)].reshape(9 * chans, width)
        full = jnp.dot(weight[...], rows, preferred_element_type=F32)
        keep = width - 2 * depth
        total = full[0:chans, 0:keep]
        total += full[chans : 2 * chans, depth : depth + keep]
        total += full[2 * chans : 3 * chans, 2 * depth : 2 * depth + keep]
        return total

    def grad(slot, delta, stack, x, first):
        width = (cy + 2) * depth
        rows = stack[pl.ds(x, 3), :, first * depth : first * depth + width].reshape(9 * chans, width)
        shifted = []
        for b in range(3):
            parts = []
            if b:
                parts.append(jnp.zeros((chans, b * depth), BF))
            parts.append(delta)
            if b < 2:
                parts.append(jnp.zeros((chans, (2 - b) * depth), BF))
            shifted.append(jnp.concatenate(parts, axis=1))
        left = jnp.concatenate(shifted, axis=0)
        gw_ref[slot, :, 0 : 9 * chans] += lax.dot_general(
            left, rows, (((1,), (1,)), ((), ())), preferred_element_type=F32
        )
        bias_acc[slot] += delta.astype(F32)

    each = g_ref.shape[3]

    def pack(slot):
        total = jnp.sum(bias_acc[slot], axis=1, keepdims=True)
        gw_ref[slot, 0:chans, 9 * chans :] = jnp.broadcast_to(
            total, (chans, gw_ref.shape[2] - 9 * chans)
        )
        for n in range(nx * ny):
            first = min(n * each, 3 * chans - each)
            g_ref[slot, n // nx, n % nx] = gw_ref[slot, first : first + each].astype(BF)

    def sum_copies(slot, phase):
        out = []
        along_y = phase in (0, 3)
        for k in range(1, ny if along_y else nx):
            peer = peer_y(k) if along_y else peer_x(k)
            if phase == 0:
                src, dst = g_ref.at[slot, peer], r1.at[slot, k]
            elif phase == 1:
                src, dst = h.at[slot, peer], r2.at[slot, k]
            elif phase == 2:
                src = dst = o_ref.at[slot, gy, gx]
            else:
                src = dst = o_ref.at[slot, gy]
            ss, rs = (sum_send_y, sum_recv_y) if along_y else (sum_send_x, sum_recv_x)
            out.append(pltpu.make_async_remote_copy(
                src_ref=src, dst_ref=dst,
                send_sem=ss.at[slot, phase // 2, k], recv_sem=rs.at[slot, phase // 2, k],
                device_id=(gx, peer) if along_y else (peer, gy), device_id_type=MESH,
            ))
        return out

    def sum_start(slot, phase):
        for copy in sum_copies(slot, phase):
            copy.start()

    def sum_finish(slot, phase):
        for copy in sum_copies(slot, phase):
            copy.wait_send()
            copy.wait_recv()
        if phase == 0:
            part = g_ref[slot, gy].astype(F32)
            for k in range(1, ny):
                part += r1[slot, k].astype(F32)
            h[slot] = part.astype(BF)
        if phase == 1:
            full = h[slot, gx].astype(F32)
            for k in range(1, nx):
                full += r2[slot, k].astype(F32)
            o_ref[slot, gy, gx] = full.astype(BF)

    gw_ref[...] = jnp.zeros_like(gw_ref)
    bias_acc[...] = jnp.zeros_like(bias_acc)

    @pl.loop(0, cx)
    def _(x):
        mask = mask_row(x + HALO, HALO, cy)
        put(s1, x + HALO, jnp.where(mask > 0, tiles(own_f, x, 0, cy).astype(F32), 0.0), HALO)

    finish(0)
    put_halo(s1, wide_f)

    @pl.loop(0, cx + 2)
    def _(x):
        mask = mask_row(x + 1, 1, cy + 2)
        pre = conv(w1_ref, s1, x) + b_ref[:, 0:1]
        put(s2, x, jnp.where(mask > 0, jnp.maximum(pre, 0.0), 0.0))

    @pl.loop(0, cx)
    def _(x):
        mask = mask_row(x + 2, 2, cy)
        pre = conv(w2_ref, s2, x) + b_ref[:, 1:2]
        vals, hits = [], []
        for y in range(cy):
            pooled = p_ref[x // 2, y // 2].astype(F32)
            code = (4 * (x % 2) + 2 * (y % 2) + lane_odd).astype(F32)
            vals.append(pooled[0:chans])
            hits.append(jnp.where(pooled[chans : 2 * chans] == code, 1.0, 0.0))
        up = jnp.concatenate(vals, axis=1)
        hit = jnp.concatenate(hits, axis=1) * mask
        chosen = jnp.where(pre > 0, hit, 0.0)
        delta = jnp.where(chosen > 0, up, 0.0)
        rounded = delta.astype(BF)
        for y in range(cy):
            wide_d[x + HALO, y + HALO] = rounded[:, y * depth : (y + 1) * depth]
        put(s3, x + HALO, delta, HALO)

    send(1)

    @pl.loop(0, cx)
    def _(x):
        delta = s3[x + HALO, chans : 2 * chans, HALO * depth : (HALO + cy) * depth]
        grad(1, delta, s2, x, 0)

    pack(1)
    finish(1)
    sum_start(1, 0)
    put_halo(s3, wide_d)

    @pl.loop(0, cx + 2)
    def _(x):
        back = conv(w2b_ref, s3, x)
        hidden = s2[x, chans : 2 * chans, :].astype(F32)
        put(s4, x, jnp.where(hidden > 0, back, 0.0))

    sum_finish(1, 0)
    sum_start(1, 1)

    @pl.loop(0, cx)
    def _(x):
        delta = s4[x + 1, chans : 2 * chans, depth : (1 + cy) * depth]
        grad(0, delta, s1, x + 1, 1)

    pack(0)
    sum_start(0, 0)
    sum_finish(1, 1)
    sum_start(1, 2)

    def last(x):
        mask = mask_row(x + 2, 2, cy)
        back = conv(w1b_ref, s4, x)
        out = jnp.where(mask > 0, back, 0.0).astype(BF)
        for y in range(cy):
            gin_ref[x, y] = out[:, y * depth : (y + 1) * depth]

    pl.loop(0, cx // 2)(last)
    sum_finish(0, 0)
    sum_start(0, 1)
    sum_finish(1, 2)
    sum_start(1, 3)
    pl.loop(cx // 2, cx)(last)
    sum_finish(0, 1)
    sum_start(0, 2)
    sum_finish(0, 2)
    sum_start(0, 3)
    sum_finish(1, 3)
    sum_finish(0, 3)


def rows_of(weight):
    channels = weight.shape[0]
    return weight.transpose(2, 0, 1, 3, 4).reshape(3 * channels, -1)


def flipped(weight):
    return jnp.flip(weight, (1, 2, 3)).transpose(4, 1, 2, 3, 0)


def vmem(count):
    return [pl.BlockSpec(memory_space=pltpu.VMEM)] * count


def body(features, occupancy, weight_one, bias_one, weight_two, bias_two, grad_pooled, pool_choice):
    chans, cx, cy, depth = features.shape
    nx, ny = lax.axis_size("gx"), lax.axis_size("gy")
    brick_x, brick_y = cx // 8, cy // 8
    padded_flags = jnp.pad(occupancy, ((1, 1), (1, 1), (0, 0)))
    flags = lax.dynamic_slice(
        padded_flags,
        (lax.axis_index("gx") * brick_x, lax.axis_index("gy") * brick_y, jnp.int32(0)),
        (brick_x + 2, brick_y + 2, occupancy.shape[2]),
    )
    mz = jnp.repeat(flags, 8, axis=2).astype(F32)
    own_f = features.transpose(1, 2, 0, 3)
    spread = np.repeat(np.eye(depth // 2, dtype=np.float32), 2, axis=1)
    both = jnp.concatenate([grad_pooled, pool_choice.astype(BF)], axis=0)
    both = jnp.dot(both, jnp.asarray(spread, BF), preferred_element_type=F32).astype(BF)
    own_p = both.transpose(1, 2, 0, 3)

    lanes = -(-(9 * chans + 1) // 128) * 128
    each = -(-3 * chans // (nx * ny))
    gin, summed = pl.pallas_call(
        functools.partial(main_kernel, nx, ny, cx, cy, depth, chans),
        out_shape=(
            jax.ShapeDtypeStruct((cx, cy, chans, depth), BF),
            jax.ShapeDtypeStruct((2, ny, nx, each, lanes), BF),
        ),
        in_specs=vmem(8),
        out_specs=tuple(vmem(2)),
        scratch_shapes=[
            pltpu.VMEM((cx + 4, cy + 4, chans, depth), BF),
            pltpu.VMEM((cx + 4, cy + 4, chans, depth), BF),
            pltpu.VMEM((cx + 4, 3 * chans, (cy + 4) * depth), BF),
            pltpu.VMEM((cx + 2, 3 * chans, (cy + 2) * depth), BF),
            pltpu.VMEM((cx + 4, 3 * chans, (cy + 4) * depth), BF),
            pltpu.VMEM((cx + 2, 3 * chans, (cy + 2) * depth), BF),
            pltpu.VMEM((2, chans, cy * depth), F32),
            pltpu.VMEM((2, 3 * chans, lanes), F32),
            pltpu.VMEM((2, ny, nx, each, lanes), BF),
            pltpu.VMEM((2, ny, nx, each, lanes), BF),
            pltpu.VMEM((2, nx, each, lanes), BF),
            pltpu.VMEM((2, nx, each, lanes), BF),
            pltpu.SemaphoreType.DMA((2, 8)),
            pltpu.SemaphoreType.DMA((2, 8)),
            pltpu.SemaphoreType.DMA((2, 2, nx)),
            pltpu.SemaphoreType.DMA((2, 2, nx)),
            pltpu.SemaphoreType.DMA((2, 2, ny)),
            pltpu.SemaphoreType.DMA((2, 2, ny)),
        ],
        compiler_params=pltpu.CompilerParams(
            collective_id=0, has_side_effects=True, vmem_limit_bytes=48 * 2**20
        ),
        name="main",
    )(
        own_f, own_p, mz,
        rows_of(weight_one), rows_of(weight_two),
        rows_of(flipped(weight_two)), rows_of(flipped(weight_one)),
        jnp.stack([bias_one, bias_two], axis=1),
    )

    total_cells = cx * nx * cy * ny * depth
    scale = 1.0 / math.sqrt(total_cells)
    sums = summed.astype(F32).reshape(2, -1, lanes)[:, : 3 * chans] * scale
    grads = sums[:, :, : 9 * chans].reshape(2, 3, chans, 3, 3, chans).transpose(0, 2, 3, 1, 4, 5)
    biases = sums[:, :chans, 9 * chans]
    grad_input = gin.transpose(2, 0, 1, 3)
    return grad_input, grads[0], biases[0], grads[1], biases[1]


def solution(mesh):
    placed = (
        P(None, "gx", "gy", None),
        P(),
        P(),
        P(),
        P(),
        P(),
        P(None, "gx", "gy", None),
        P(None, "gx", "gy", None),
    )
    return jax.shard_map(
        body,
        mesh=mesh,
        in_specs=placed,
        out_specs=(P(None, "gx", "gy", None), P(), P(), P(), P()),
        check_vma=False,
    )
```

time: 79 us -> 69.6 us (0.88)
  Pallas kernels: 64.5 us -> 56.9 us
  local copies, waits for them, and re-layouts: 9.6 us -> 8.1 us
    pallas_call x1 -> x0, Pallas kernels: 26.9 us -> none  [body(): pl.pallas_call(functools.partial(sum_kernel, nx, ny), out_shape=jax.Shape...]
    pallas_call x1, Pallas kernels: 37.6 us -> 56.9 us  [body(): pl.pallas_call(functools.partial(main_kernel, nx, ny, cx, cy, depth, chan...]
    broadcast_in_dim x2 -> x0, local copies, waits for them, and re-layouts: 1.47 us -> none  [the longest x1 0.74 us: body(): bias_one[:, None]]
    unnamed x10 -> x11, local copies, waits for them, and re-layouts: 2.82 us -> 4.07 us
    transpose x1 -> x0, local copies, waits for them, and re-layouts: 0.94 us -> none  [body(): grad_input = gin.reshape(cx, chans, cy, depth).transpose(1, 0, 2, 3)]
    mul x1, other arithmetic: 0.96 us -> 0.09 us  [body(): sums = summed.astype(F32).reshape(2, -1, lanes)[:, :3 * chans] * scale]
where the time goes in v3:
time: 69.6 us; the launch traced here: 69.3 us
  Pallas kernels  56.9 us (82%)
  local copies, waits for them, and re-layouts  8.1 us (12%)
  other arithmetic  2.59 us (4%)
  matrix products  0.93 us (1%)
  between operations  0.79 us (1%)
    pallas_call x1, Pallas kernels, body(): pl.pallas_call(functools.partial(main_kernel, nx, ny, cx, cy, depth, chan...  56.9 us
    unnamed x11, local copies, waits for them, and re-layouts  4.07 us

profile of v3, /device:TPU:0, one launch (start us, length us, event | category | flops | bytes accessed | tf_op | source)
XLA Modules:
  0.0 69.3 jit_solution(7391941941294319902)
XLA Ops:
  0.6 0.0 copy-start.1
  0.6 0.7 %pad_maximum_fusion = f32[32,2]{0,1:T(2,128)S(1)} fusion(f32[32,1]{0,1:T(1,128)} %bitcast.34, f32[32,1]{0,1:T(1,128)} %bitcast.35), kind=kLoop, calls=%fused_computation.16 | loop fusion | flops 64 | bytes 512 | tf_op jit(solution)/shard_map/stack | solution.py:386
  1.4 0.7 %fusion.4 = f32[3,3,16]{2,1,0:T(4,128)S(1)} fusion(s32[]{:T(128)S(6)} %select_n.6, s32[]{:T(128)S(6)} %select_n.7, s32[8,4,16]{2,1,0:T(4,128)} %param.10), kind=kLoop, calls=%fused_computation.15 | loop fusion | flops 144 | bytes 2632 | tf_op jit(solution)/shard_map/convert_element_type | solution.py:341
  2.1 0.1 copy.61.b_ref
  2.2 0.1 broadcast_in_dim.3
  2.2 0.1 convert_element_type.22.mz_ref
  2.4 0.9 %copy.56 = bf16[32,4,4,64]{3,0,2,1:T(8,128)(2,1)S(1)} copy(bf16[32,4,4,64]{3,2,1,0:T(4,128)(2,1)} %param.15) | data formatting | bytes 131072 | tf_op args[6]
  3.3 0.0 copy-start
  3.3 1.1 %copy_convert_fusion = bf16[32,4,4,64]{3,0,2,1:T(8,128)(2,1)S(1)} fusion(s32[32,4,4,64]{3,2,1,0:T(4,128)} %param.16), kind=kLoop, calls=%fused_computation.9 | loop fusion | flops 32768 | bytes 196608 | tf_op jit(solution)/shard_map/convert_element_type | solution.py:344
  4.4 0.9 %fusion.p_ref = bf16[4,4,64,128]{3,2,1,0:T(8,128)(2,1)S(1)} fusion(bf16[64,128,1,1]{1,0,3,2:T(8,128)(2,1)} %constant.24, bf16[32,4,4,64]{3,0,2,1:T(8,128)(2,1)S(1)} %copy_convert_fusion, bf16[32,4,4,64]{3,0,2,1:T(8,128)(2,1)S(1)} %copy.56), kind=kOutput, calls=%fused_computation.1 | convolution fusion | flops 17170432 | bytes 409600 | tf_op jit(solution)/shard_map/dot_general | solution.py:345
  5.3 0.0 copy-done.1
  5.4 0.2 copy.60
  5.6 0.2 reshape.37.w1b_ref
  5.7 0.0 copy-done
  5.8 0.2 copy.59
  6.0 0.0 copy-start.2
  6.0 0.2 reshape.36.w2b_ref
  6.2 0.2 copy.58
  6.3 0.2 reshape.35.w2_ref
  6.5 0.2 copy.57
  6.7 0.2 reshape.34.w1_ref
  6.9 0.1 copy-done.2
  7.0 0.3 copy.70
  7.4 56.9 %main.1 = (bf16[8,8,32,128]{3,2,1,0:T(8,128)(2,1)S(1)}, bf16[2,4,8,3,384]{4,3,2,1,0:T(4,128)(2,1)S(1)}) custom-call(bf16[8,8,32,128]{3,2,1,0:T(8,128)(2,1)S(1)} %bitcast.27, bf16[4,4,64,128]{3,2,1,0:T(8,128)(2,1)S(1)} %fusion.p_ref, f32[3,3,128]{2,1,0:T(4,128)S(1)} %convert_element_type.22.mz_ref, bf16[96,288]{1,0:T(8,128)(2,1)S(1)} %reshape.34.w1_ref, ...), custom_call_target="tpu_custom_call" | custom-call | tf_op jit(solution)/shard_map/main/pallas_call | solution.py:350
  64.3 1.0 %copy.64 = bf16[32,8,8,128]{3,2,1,0:T(8,128)(2,1)} copy(bf16[32,8,8,128]{3,0,2,1:T(8,128)(2,1)S(1)} %bitcast.28) | data formatting | bytes 1048576
  65.3 0.1 convert_multiply_fusion
  65.4 0.2 copy.62
  65.6 1.4 %slice_reduce_fusion = (f32[32]{0:T(128)}, f32[32]{0:T(128)}) fusion(f32[2,96,384]{2,0,1:T(2,128)S(1)} %bitcast.30), kind=kLoop, calls=%fused_computation.13 | loop fusion | bytes 512 | tf_op jit(solution)/shard_map/slice | solution.py:395
  67.0 0.5 reshape.38
  67.5 0.2 slice_bitcast_fusion
  67.7 0.8 %copy.66 = f32[32,3,3,3,32]{4,0,3,2,1:T(8,128)} copy(f32[32,3,3,3,32]{4,3,1,0,2:T(4,128)S(1)} %get-tuple-element.31) | data formatting | bytes 221184
  68.5 0.8 %copy.65 = f32[32,3,3,3,32]{4,0,3,2,1:T(8,128)} copy(f32[32,3,3,3,32]{4,3,1,0,2:T(4,128)S(1)} %get-tuple-element.32) | data formatting | bytes 221184
  (3 shorter events, 0.1 us)
Async XLA Ops:
  0.6 4.7 %copy-start.1 = (bf16[32,3,3,3,32]{4,0,3,2,1:T(8,128)(2,1)S(1)}, bf16[32,3,3,3,32]{4,0,3,2,1:T(8,128)(2,1)}, u32[]{:S(2)}) copy-start(bf16[32,3,3,3,32]{4,0,3,2,1:T(8,128)(2,1)} %param.11) | copy-start | bytes 165892
  3.3 2.5 %copy-start = (bf16[32,3,3,3,32]{4,0,3,2,1:T(8,128)(2,1)S(1)}, bf16[32,3,3,3,32]{4,0,3,2,1:T(8,128)(2,1)}, u32[]{:S(2)}) copy-start(bf16[32,3,3,3,32]{4,0,3,2,1:T(8,128)(2,1)} %param.13) | copy-start | bytes 165892
  6.0 1.0 %copy-start.2 = (bf16[32,8,8,128]{3,2,1,0:T(8,128)(2,1)S(1)}, bf16[32,8,8,128]{3,2,1,0:T(8,128)(2,1)}, u32[]{:S(2)}) copy-start(bf16[32,8,8,128]{3,2,1,0:T(8,128)(2,1)} %param.9) | copy-start | bytes 1572868

commit v4 on v3

--- a/solution.py
+++ b/solution.py
@@ -104,17 +104,28 @@
 
     send(0)
 
+    same = lax.broadcasted_iota(jnp.int32, (chans, chans), 0) == lax.broadcasted_iota(
+        jnp.int32, (chans, chans), 1
+    )
+
+    def column(n):
+        return jnp.sum(jnp.where(same, b_ref[n : n + 1, :], 0.0), axis=1, keepdims=True)
+
+    bias_one, bias_two = column(0), column(1)
     lane = lax.broadcasted_iota(jnp.int32, (1, depth), 1)
     not_first = lane != 0
     not_last = lane != depth - 1
     lane_odd = lane % 2
 
     def mask_row(x, first, count):
-        flags = mz_ref[(x + 8 - HALO) // 8]
+        brick = gx * (cx // 8) + (x + 8 - HALO) // 8
+        flags = {}
         parts = []
         for y in range(first, first + count):
             by = (y + 8 - HALO) // 8
-            parts.append(flags[by : by + 1, :])
+            if by not in flags:
+                flags[by] = mz_ref[brick, pl.ds(gy * (cy // 8) + by, 1), :]
+            parts.append(flags[by])
         return jnp.concatenate(parts, axis=1)
 
     def put(stack, x, value, first=0):
@@ -139,11 +150,11 @@
         put(stack, x, jnp.where(mask > 0, tiles(ref, x, first, count).astype(F32), 0.0), first)
 
     def put_halo(stack, ref):
-        @pl.loop(0, 2 * HALO)
+        @pl.loop(0, 2 * HALO, unroll=2)
         def _(n):
             put_cells(stack, ref, n + cx * (n // HALO), 0, cy + 2 * HALO)
 
-        @pl.loop(HALO, HALO + cx)
+        @pl.loop(HALO, HALO + cx, unroll=2)
         def _(x):
             put_cells(stack, ref, x, 0, HALO)
             put_cells(stack, ref, x, HALO + cy, HALO)
@@ -230,7 +241,7 @@
     gw_ref[...] = jnp.zeros_like(gw_ref)
     bias_acc[...] = jnp.zeros_like(bias_acc)
 
-    @pl.loop(0, cx)
+    @pl.loop(0, cx, unroll=2)
     def _(x):
         mask = mask_row(x + HALO, HALO, cy)
         put(s1, x + HALO, jnp.where(mask > 0, tiles(own_f, x, 0, cy).astype(F32), 0.0), HALO)
@@ -238,16 +249,16 @@
     finish(0)
     put_halo(s1, wide_f)
 
-    @pl.loop(0, cx + 2)
+    @pl.loop(0, cx + 2, unroll=2)
     def _(x):
         mask = mask_row(x + 1, 1, cy + 2)
-        pre = conv(w1_ref, s1, x) + b_ref[:, 0:1]
+        pre = conv(w1_ref, s1, x) + bias_one
         put(s2, x, jnp.where(mask > 0, jnp.maximum(pre, 0.0), 0.0))
 
-    @pl.loop(0, cx)
+    @pl.loop(0, cx, unroll=2)
     def _(x):
         mask = mask_row(x + 2, 2, cy)
-        pre = conv(w2_ref, s2, x) + b_ref[:, 1:2]
+        pre = conv(w2_ref, s2, x) + bias_two
         vals, hits = [], []
         for y in range(cy):
             pooled = p_ref[x // 2, y // 2].astype(F32)
@@ -265,7 +276,7 @@
 
     send(1)
 
-    @pl.loop(0, cx)
+    @pl.loop(0, cx, unroll=2)
     def _(x):
         delta = s3[x + HALO, chans : 2 * chans, HALO * depth : (HALO + cy) * depth]
         grad(1, delta, s2, x, 0)
@@ -275,7 +286,7 @@
     sum_start(1, 0)
     put_halo(s3, wide_d)
 
-    @pl.loop(0, cx + 2)
+    @pl.loop(0, cx + 2, unroll=2)
     def _(x):
         back = conv(w2b_ref, s3, x)
         hidden = s2[x, chans : 2 * chans, :].astype(F32)
@@ -284,7 +295,7 @@
     sum_finish(1, 0)
     sum_start(1, 1)
 
-    @pl.loop(0, cx)
+    @pl.loop(0, cx, unroll=2)
     def _(x):
         delta = s4[x + 1, chans : 2 * chans, depth : (1 + cy) * depth]
         grad(0, delta, s1, x + 1, 1)
@@ -301,12 +312,12 @@
         for y in range(cy):
             gin_ref[x, y] = out[:, y * depth : (y + 1) * depth]
 
-    pl.loop(0, cx // 2)(last)
+    pl.loop(0, cx // 2, unroll=2)(last)
     sum_finish(0, 0)
     sum_start(0, 1)
     sum_finish(1, 2)
     sum_start(1, 3)
-    pl.loop(cx // 2, cx)(last)
+    pl.loop(cx // 2, cx, unroll=2)(last)
     sum_finish(0, 1)
     sum_start(0, 2)
     sum_finish(0, 2)
@@ -331,14 +342,8 @@
 def body(features, occupancy, weight_one, bias_one, weight_two, bias_two, grad_pooled, pool_choice):
     chans, cx, cy, depth = features.shape
     nx, ny = lax.axis_size("gx"), lax.axis_size("gy")
-    brick_x, brick_y = cx // 8, cy // 8
-    padded_flags = jnp.pad(occupancy, ((1, 1), (1, 1), (0, 0)))
-    flags = lax.dynamic_slice(
-        padded_flags,
-        (lax.axis_index("gx") * brick_x, lax.axis_index("gy") * brick_y, jnp.int32(0)),
-        (brick_x + 2, brick_y + 2, occupancy.shape[2]),
-    )
-    mz = jnp.repeat(flags, 8, axis=2).astype(F32)
+    flags = jnp.pad(occupancy, ((1, 1), (1, 1), (0, 0))).astype(F32)
+    mz = jnp.repeat(flags, 8, axis=2)
     own_f = features.transpose(1, 2, 0, 3)
     spread = np.repeat(np.eye(depth // 2, dtype=np.float32), 2, axis=1)
     both = jnp.concatenate([grad_pooled, pool_choice.astype(BF)], axis=0)
@@ -383,14 +388,14 @@
         own_f, own_p, mz,
         rows_of(weight_one), rows_of(weight_two),
         rows_of(flipped(weight_two)), rows_of(flipped(weight_one)),
-        jnp.stack([bias_one, bias_two], axis=1),
+        jnp.stack([bias_one, bias_two]),
     )
 
     total_cells = cx * nx * cy * ny * depth
     scale = 1.0 / math.sqrt(total_cells)
     sums = summed.astype(F32).reshape(2, -1, lanes)[:, : 3 * chans] * scale
     grads = sums[:, :, : 9 * chans].reshape(2, 3, chans, 3, 3, chans).transpose(0, 2, 3, 1, 4, 5)
-    biases = sums[:, :chans, 9 * chans]
+    biases = summed[..., 9 * chans].astype(F32).reshape(2, -1)[:, :chans] * scale
     grad_input = gin.transpose(2, 0, 1, 3)
     return grad_input, grads[0], biases[0], grads[1], biases[1]
 

time: 69.6 us -> 64.8 us (0.931)
  Pallas kernels: 56.9 us -> 52.4 us
    pallas_call x1, Pallas kernels: 56.9 us -> 52.4 us  [body(): pl.pallas_call(functools.partial(main_kernel, nx, ny, cx, cy, depth, chan...]
    slice x1, local copies, waits for them, and re-layouts: 1.36 us -> 0.25 us  [body(): summed[..., 9 * chans].astype(F32).reshape(2, -1)[:, :chans] * scale]
where the time goes in v4:
time: 64.8 us; the launch traced here: 64.4 us
  Pallas kernels  52.4 us (81%)
  local copies, waits for them, and re-layouts  7.69 us (12%)
  other arithmetic  2.62 us (4%)
  matrix products  0.93 us (1%)
  between operations  0.81 us (1%)
    pallas_call x1, Pallas kernels, body(): pl.pallas_call(functools.partial(main_kernel, nx, ny, cx, cy, depth, chan...  52.4 us
    unnamed x11, local copies, waits for them, and re-layouts  3.97 us

profile of v4, /device:TPU:0, one launch (start us, length us, event | category | flops | bytes accessed | tf_op | source)
XLA Modules:
  0.0 64.4 jit_solution(1986282952203423849)
XLA Ops:
  0.6 0.0 copy-start.1
  0.6 0.7 %pad_maximum_fusion.b_ref = f32[2,32]{1,0:T(2,128)S(1)} fusion(f32[1,32]{1,0:T(1,128)} %bitcast.39, f32[1,32]{1,0:T(1,128)} %bitcast.40), kind=kLoop, calls=%fused_computation.14 | loop fusion | flops 64 | bytes 512 | tf_op jit(solution)/shard_map/stack | solution.py:391
  1.4 0.7 %pad_convert_fusion = f32[10,6,16]{2,1,0:T(8,128)S(1)} fusion(s32[8,4,16]{2,1,0:T(4,128)} %param.10), kind=kLoop, calls=%fused_computation.13 | loop fusion | flops 960 | bytes 5888 | tf_op jit(solution)/shard_map/convert_element_type | solution.py:345
  2.1 0.9 %copy.24 = bf16[32,4,4,64]{3,0,2,1:T(8,128)(2,1)S(1)} copy(bf16[32,4,4,64]{3,2,1,0:T(4,128)(2,1)} %param.15) | data formatting | bytes 131072 | tf_op args[6]
  3.0 0.0 copy-start
  3.1 1.1 %copy_convert_fusion = bf16[32,4,4,64]{3,0,2,1:T(8,128)(2,1)S(1)} fusion(s32[32,4,4,64]{3,2,1,0:T(4,128)} %param.16), kind=kLoop, calls=%fused_computation.9 | loop fusion | flops 32768 | bytes 196608 | tf_op jit(solution)/shard_map/convert_element_type | solution.py:349
  4.1 0.9 %fusion.p_ref = bf16[4,4,64,128]{3,2,1,0:T(8,128)(2,1)S(1)} fusion(bf16[64,128,1,1]{1,0,3,2:T(8,128)(2,1)} %constant.12, bf16[32,4,4,64]{3,0,2,1:T(8,128)(2,1)S(1)} %copy_convert_fusion, bf16[32,4,4,64]{3,0,2,1:T(8,128)(2,1)S(1)} %copy.24), kind=kOutput, calls=%fused_computation.1 | convolution fusion | flops 17170432 | bytes 409600 | tf_op jit(solution)/shard_map/dot_general | solution.py:350
  5.1 0.0 copy-done.1
  5.1 0.2 copy.28
  5.3 0.2 reshape.39.w1b_ref
  5.5 0.2 copy.27
  5.7 0.2 reshape.38.w2b_ref
  5.9 0.2 copy.26
  6.1 0.0 copy-start.2
  6.1 0.2 reshape.37.w2_ref
  6.3 0.2 copy.25
  6.4 0.2 reshape.36.w1_ref
  6.6 0.2 broadcast_in_dim.3
  6.8 0.3 reshape.35.mz_ref
  7.1 0.0 copy-done.2
  7.1 0.3 copy.37
  7.5 52.4 %main.1 = (bf16[8,8,32,128]{3,2,1,0:T(8,128)(2,1)S(1)}, bf16[2,4,8,3,384]{4,3,2,1,0:T(4,128)(2,1)S(1)}) custom-call(bf16[8,8,32,128]{3,2,1,0:T(8,128)(2,1)S(1)} %bitcast.33, bf16[4,4,64,128]{3,2,1,0:T(8,128)(2,1)S(1)} %fusion.p_ref, f32[10,6,128]{2,1,0:T(8,128)S(1)} %reshape.35.mz_ref, bf16[96,288]{1,0:T(8,128)(2,1)S(1)} %reshape.36.w1_ref, ...), custom_call_target="tpu_custom_call" | custom-call | tf_op jit(solution)/shard_map/main/pallas_call | solution.py:355
  59.8 1.0 %copy.31 = bf16[32,8,8,128]{3,2,1,0:T(8,128)(2,1)} copy(bf16[32,8,8,128]{3,0,2,1:T(8,128)(2,1)S(1)} %bitcast.34) | data formatting | bytes 1048576
  60.8 0.2 slice_reduce_fusion
  61.1 0.1 convert_element_type.26
  61.2 0.5 slice_bitcast_fusion.2
  61.7 0.1 convert_multiply_fusion
  61.8 0.2 copy.29
  62.1 0.5 reshape.40
  62.6 0.2 slice_bitcast_fusion
  62.8 0.8 %copy.33 = f32[32,3,3,3,32]{4,0,3,2,1:T(8,128)} copy(f32[32,3,3,3,32]{4,3,1,0,2:T(4,128)S(1)} %get-tuple-element.19) | data formatting | bytes 221184
  63.6 0.8 %copy.32 = f32[32,3,3,3,32]{4,0,3,2,1:T(8,128)} copy(f32[32,3,3,3,32]{4,3,1,0,2:T(4,128)S(1)} %get-tuple-element.20) | data formatting | bytes 221184
  (5 shorter events, 0.1 us)
Async XLA Ops:
  0.6 4.4 %copy-start.1 = (bf16[32,3,3,3,32]{4,0,3,2,1:T(8,128)(2,1)S(1)}, bf16[32,3,3,3,32]{4,0,3,2,1:T(8,128)(2,1)}, u32[]{:S(2)}) copy-start(bf16[32,3,3,3,32]{4,0,3,2,1:T(8,128)(2,1)} %param.11) | copy-start | bytes 165892
  3.0 2.5 %copy-start = (bf16[32,3,3,3,32]{4,0,3,2,1:T(8,128)(2,1)S(1)}, bf16[32,3,3,3,32]{4,0,3,2,1:T(8,128)(2,1)}, u32[]{:S(2)}) copy-start(bf16[32,3,3,3,32]{4,0,3,2,1:T(8,128)(2,1)} %param.13) | copy-start | bytes 165892
  6.1 1.0 %copy-start.2 = (bf16[32,8,8,128]{3,2,1,0:T(8,128)(2,1)S(1)}, bf16[32,8,8,128]{3,2,1,0:T(8,128)(2,1)}, u32[]{:S(2)}) copy-start(bf16[32,8,8,128]{3,2,1,0:T(8,128)(2,1)} %param.9) | copy-start | bytes 1572868

commit v5 on v4

--- a/solution.py
+++ b/solution.py
@@ -11,9 +11,17 @@
 
 MESH = pl.DeviceIdType.MESH
 HALO = 2
-SIDES = tuple((sx, sy) for sx in (-1, 0, 1) for sy in (-1, 0, 1) if (sx, sy) != (0, 0))
+SIDES = ((0, -1), (0, 1), (-1, 0), (1, 0), (-1, -1), (-1, 1), (1, -1), (1, 1))
 BF = jnp.bfloat16
 F32 = jnp.float32
+
+
+def each_row(first, end):
+    def run(step):
+        for row in range(first, end):
+            step(row)
+
+    return run
 
 
 def edge(side, cells):
@@ -150,11 +158,11 @@
         put(stack, x, jnp.where(mask > 0, tiles(ref, x, first, count).astype(F32), 0.0), first)
 
     def put_halo(stack, ref):
-        @pl.loop(0, 2 * HALO, unroll=2)
+        @each_row(0, 2 * HALO)
         def _(n):
             put_cells(stack, ref, n + cx * (n // HALO), 0, cy + 2 * HALO)
 
-        @pl.loop(HALO, HALO + cx, unroll=2)
+        @each_row(HALO, HALO + cx)
         def _(x):
             put_cells(stack, ref, x, 0, HALO)
             put_cells(stack, ref, x, HALO + cy, HALO)
@@ -241,7 +249,7 @@
     gw_ref[...] = jnp.zeros_like(gw_ref)
     bias_acc[...] = jnp.zeros_like(bias_acc)
 
-    @pl.loop(0, cx, unroll=2)
+    @each_row(0, cx)
     def _(x):
         mask = mask_row(x + HALO, HALO, cy)
         put(s1, x + HALO, jnp.where(mask > 0, tiles(own_f, x, 0, cy).astype(F32), 0.0), HALO)
@@ -249,13 +257,13 @@
     finish(0)
     put_halo(s1, wide_f)
 
-    @pl.loop(0, cx + 2, unroll=2)
+    @each_row(0, cx + 2)
     def _(x):
         mask = mask_row(x + 1, 1, cy + 2)
         pre = conv(w1_ref, s1, x) + bias_one
         put(s2, x, jnp.where(mask > 0, jnp.maximum(pre, 0.0), 0.0))
 
-    @pl.loop(0, cx, unroll=2)
+    @each_row(0, cx)
     def _(x):
         mask = mask_row(x + 2, 2, cy)
         pre = conv(w2_ref, s2, x) + bias_two
@@ -276,7 +284,7 @@
 
     send(1)
 
-    @pl.loop(0, cx, unroll=2)
+    @each_row(0, cx)
     def _(x):
         delta = s3[x + HALO, chans : 2 * chans, HALO * depth : (HALO + cy) * depth]
         grad(1, delta, s2, x, 0)
@@ -286,7 +294,7 @@
     sum_start(1, 0)
     put_halo(s3, wide_d)
 
-    @pl.loop(0, cx + 2, unroll=2)
+    @each_row(0, cx + 2)
     def _(x):
         back = conv(w2b_ref, s3, x)
         hidden = s2[x, chans : 2 * chans, :].astype(F32)
@@ -295,7 +303,7 @@
     sum_finish(1, 0)
     sum_start(1, 1)
 
-    @pl.loop(0, cx, unroll=2)
+    @each_row(0, cx)
     def _(x):
         delta = s4[x + 1, chans : 2 * chans, depth : (1 + cy) * depth]
         grad(0, delta, s1, x + 1, 1)
@@ -312,12 +320,12 @@
         for y in range(cy):
             gin_ref[x, y] = out[:, y * depth : (y + 1) * depth]
 
-    pl.loop(0, cx // 2, unroll=2)(last)
+    each_row(0, cx // 2)(last)
     sum_finish(0, 0)
     sum_start(0, 1)
     sum_finish(1, 2)
     sum_start(1, 3)
-    pl.loop(cx // 2, cx, unroll=2)(last)
+    each_row(cx // 2, cx)(last)
     sum_finish(0, 1)
     sum_start(0, 2)
     sum_finish(0, 2)

time: 64.8 us -> 62.5 us (0.965)
  Pallas kernels: 52.4 us -> 50.1 us
    pallas_call x1, Pallas kernels: 52.4 us -> 50.1 us  [body(): pl.pallas_call(functools.partial(main_kernel, nx, ny, cx, cy, depth, chan...]
where the time goes in v5:
time: 62.5 us; the launch traced here: 62.1 us
  Pallas kernels  50.1 us (80%)
  local copies, waits for them, and re-layouts  7.69 us (12%)
  other arithmetic  2.62 us (4%)
  matrix products  0.93 us (1%)
  between operations  0.81 us (1%)
    pallas_call x1, Pallas kernels, body(): pl.pallas_call(functools.partial(main_kernel, nx, ny, cx, cy, depth, chan...  50.1 us
    unnamed x11, local copies, waits for them, and re-layouts  3.97 us

profile of v5, /device:TPU:0, one launch (start us, length us, event | category | flops | bytes accessed | tf_op | source)
XLA Modules:
  0.0 62.1 jit_solution(5323106747963797401)
XLA Ops:
  0.6 0.0 copy-start.1
  0.6 0.7 %pad_maximum_fusion.b_ref = f32[2,32]{1,0:T(2,128)S(1)} fusion(f32[1,32]{1,0:T(1,128)} %bitcast.39, f32[1,32]{1,0:T(1,128)} %bitcast.40), kind=kLoop, calls=%fused_computation.14 | loop fusion | flops 64 | bytes 512 | tf_op jit(solution)/shard_map/stack | solution.py:399
  1.4 0.7 %pad_convert_fusion = f32[10,6,16]{2,1,0:T(8,128)S(1)} fusion(s32[8,4,16]{2,1,0:T(4,128)} %param.10), kind=kLoop, calls=%fused_computation.13 | loop fusion | flops 960 | bytes 5888 | tf_op jit(solution)/shard_map/convert_element_type | solution.py:353
  2.1 0.9 %copy.24 = bf16[32,4,4,64]{3,0,2,1:T(8,128)(2,1)S(1)} copy(bf16[32,4,4,64]{3,2,1,0:T(4,128)(2,1)} %param.15) | data formatting | bytes 131072 | tf_op args[6]
  3.0 0.0 copy-start
  3.1 1.1 %copy_convert_fusion = bf16[32,4,4,64]{3,0,2,1:T(8,128)(2,1)S(1)} fusion(s32[32,4,4,64]{3,2,1,0:T(4,128)} %param.16), kind=kLoop, calls=%fused_computation.9 | loop fusion | flops 32768 | bytes 196608 | tf_op jit(solution)/shard_map/convert_element_type | solution.py:357
  4.1 0.9 %fusion.p_ref = bf16[4,4,64,128]{3,2,1,0:T(8,128)(2,1)S(1)} fusion(bf16[64,128,1,1]{1,0,3,2:T(8,128)(2,1)} %constant.12, bf16[32,4,4,64]{3,0,2,1:T(8,128)(2,1)S(1)} %copy_convert_fusion, bf16[32,4,4,64]{3,0,2,1:T(8,128)(2,1)S(1)} %copy.24), kind=kOutput, calls=%fused_computation.1 | convolution fusion | flops 17170432 | bytes 409600 | tf_op jit(solution)/shard_map/dot_general | solution.py:358
  5.1 0.0 copy-done.1
  5.1 0.2 copy.28
  5.3 0.2 reshape.39.w1b_ref
  5.5 0.2 copy.27
  5.7 0.2 reshape.38.w2b_ref
  5.9 0.2 copy.26
  6.1 0.0 copy-start.2
  6.1 0.2 reshape.37.w2_ref
  6.3 0.2 copy.25
  6.4 0.2 reshape.36.w1_ref
  6.6 0.2 broadcast_in_dim.3
  6.8 0.3 reshape.35.mz_ref
  7.1 0.0 copy-done.2
  7.1 0.3 copy.37
  7.5 50.1 %main.1 = (bf16[8,8,32,128]{3,2,1,0:T(8,128)(2,1)S(1)}, bf16[2,4,8,3,384]{4,3,2,1,0:T(4,128)(2,1)S(1)}) custom-call(bf16[8,8,32,128]{3,2,1,0:T(8,128)(2,1)S(1)} %bitcast.33, bf16[4,4,64,128]{3,2,1,0:T(8,128)(2,1)S(1)} %fusion.p_ref, f32[10,6,128]{2,1,0:T(8,128)S(1)} %reshape.35.mz_ref, bf16[96,288]{1,0:T(8,128)(2,1)S(1)} %reshape.36.w1_ref, ...), custom_call_target="tpu_custom_call" | custom-call | tf_op jit(solution)/shard_map/main/pallas_call | solution.py:363
  57.6 1.0 %copy.31 = bf16[32,8,8,128]{3,2,1,0:T(8,128)(2,1)} copy(bf16[32,8,8,128]{3,0,2,1:T(8,128)(2,1)S(1)} %bitcast.34) | data formatting | bytes 1048576
  58.6 0.2 slice_reduce_fusion
  58.8 0.1 convert_element_type.26
  58.9 0.5 slice_bitcast_fusion.2
  59.5 0.1 convert_multiply_fusion
  59.6 0.2 copy.29
  59.8 0.5 reshape.40
  60.3 0.2 slice_bitcast_fusion
  60.5 0.8 %copy.33 = f32[32,3,3,3,32]{4,0,3,2,1:T(8,128)} copy(f32[32,3,3,3,32]{4,3,1,0,2:T(4,128)S(1)} %get-tuple-element.19) | data formatting | bytes 221184
  61.3 0.8 %copy.32 = f32[32,3,3,3,32]{4,0,3,2,1:T(8,128)} copy(f32[32,3,3,3,32]{4,3,1,0,2:T(4,128)S(1)} %get-tuple-element.20) | data formatting | bytes 221184
  (5 shorter events, 0.1 us)
Async XLA Ops:
  0.6 4.4 %copy-start.1 = (bf16[32,3,3,3,32]{4,0,3,2,1:T(8,128)(2,1)S(1)}, bf16[32,3,3,3,32]{4,0,3,2,1:T(8,128)(2,1)}, u32[]{:S(2)}) copy-start(bf16[32,3,3,3,32]{4,0,3,2,1:T(8,128)(2,1)} %param.11) | copy-start | bytes 165892
  3.0 2.5 %copy-start = (bf16[32,3,3,3,32]{4,0,3,2,1:T(8,128)(2,1)S(1)}, bf16[32,3,3,3,32]{4,0,3,2,1:T(8,128)(2,1)}, u32[]{:S(2)}) copy-start(bf16[32,3,3,3,32]{4,0,3,2,1:T(8,128)(2,1)} %param.13) | copy-start | bytes 165892
  6.1 1.0 %copy-start.2 = (bf16[32,8,8,128]{3,2,1,0:T(8,128)(2,1)S(1)}, bf16[32,8,8,128]{3,2,1,0:T(8,128)(2,1)}, u32[]{:S(2)}) copy-start(bf16[32,8,8,128]{3,2,1,0:T(8,128)(2,1)} %param.9) | copy-start | bytes 1572868
